TPU v7x, 128 devices: a whole 4x4x4 slice. The times are simulated.
128 devices in a mesh: ctx: 16 (over y, z), seq: 8 (over x, core).
Axes of the slice: x: 4, y: 4, z: 4, core: 2. Of those that a mesh axis runs over, the one named last changes fastest.
Arguments:
- query_matrix: bfloat16 [131072, 2048], P(('seq', 'ctx')), parts along dimension 0, may hold values from -7 to 7
- key_vectors: bfloat16 [131072, 2048], P(('seq', 'ctx')), parts along dimension 0, may hold values from -7.5 to 7.5
- value_vectors: bfloat16 [131072, 4096], P(('seq', 'ctx')), parts along dimension 0, may hold values from -6 to 6
- input_gate: float32 [8, 131072], P(None, ('seq', 'ctx')), parts along dimension 1, may hold values from -4 to 300
- forget_gate: float32 [8, 131072], P(None, ('seq', 'ctx')), parts along dimension 1, may hold values from 0 to 12.7
Outputs:
- hidden_state: bfloat16 [131072, 4096], P(('seq', 'ctx')), parts along dimension 0
- final_memory: float32 [64, 256, 512], P('seq', 'ctx'), parts along dimension 0
- final_normalizer: float32 [64, 256], P('seq', 'ctx'), parts along dimension 0
- final_stabilizer: float32 [64], P('seq'), parts along dimension 0
There are 8 independent parts, one for each index of `seq`. A program takes and returns all parts, laid end to end along the dimension named above; each array names one. Nothing has to cross between parts.
All inputs are finite; a program needn't handle non-finite values.
Results may differ from a plain program's by a relative error of at most 0.0056.
Values sent between devices are 32-bit elements; how exact they have to be, the bound alone decides.
A program may use at most 192 MiB of HBM per device.

v0:
```python
import math

import jax
import jax.numpy as jnp
from jax import lax
from jax.sharding import Mesh
from jax.sharding import PartitionSpec as P

H = 8
DQK = 256
DV = 512
CTX = ("ctx_0", "ctx_1")
SEQ_CTX = ("seq", "ctx_0", "ctx_1")


VERY_NEGATIVE = -1e30


def nothing_yet(x, identity):
    return jax.tree.map(
        lambda part, zero: jnp.zeros_like(part) + jnp.asarray(zero, part.dtype), x, identity
    )


def prefix_by_axis(x, axes, combine, identity):
    before = start = nothing_yet(x, identity)
    running = x
    for axis in reversed(axes):
        size, position = (lax.axis_size(axis), lax.axis_index(axis))
        pieces = jax.tree.map(lambda part: lax.all_gather(part, axis), running)
        inside, running = (start, start)
        for k in range(size):
            passed = k < position
            running = combine(running, jax.tree.map(lambda part: part[k], pieces))
            inside = jax.tree.map(lambda new, old: jnp.where(passed, new, old), running, inside)
        before = combine(inside, before)
    return before


def copy_for_each(x, axis):
    size = lax.axis_size(axis)
    return lax.all_to_all(jnp.broadcast_to(x[None], (size, *x.shape)), axis, 0, 0, tiled=True)


def taken_together(x, axis):
    return copy_for_each(x, axis).sum(axis=0)


def of_everyone(x, axis):
    return copy_for_each(x, axis).max(axis=0)


def summarize(key_vectors, value_vectors, input_gate, cumulated):
    decay_sum = cumulated[:, -1]
    exponent = decay_sum[:, None] - cumulated + input_gate
    stabilizer = jnp.max(exponent, axis=1)
    weight = jnp.exp(exponent - stabilizer[:, None])

    def summarize_one_head(head_index):
        key_rows = lax.dynamic_slice_in_dim(key_vectors, head_index * DQK, DQK, 1).astype(
            jnp.float32
        )
        value_rows = lax.dynamic_slice_in_dim(value_vectors, head_index * DV, DV, 1)
        scaled = key_rows * weight[head_index][:, None]
        matrix_memory = lax.dot_general(
            scaled.astype(jnp.bfloat16),
            value_rows,
            (((0,), (0,)), ((), ())),
            preferred_element_type=jnp.float32,
        )
        return (matrix_memory, jnp.sum(scaled, axis=0))

    matrix_memory, normal = lax.map(summarize_one_head, jnp.arange(H, dtype=jnp.int32))
    return (matrix_memory, normal, stabilizer, decay_sum)


def combine(earlier, later):
    first_memory, first_normal, first_stab, first_decay = earlier
    second_memory, second_normal, second_stab, second_decay = later
    stabilizer = jnp.maximum(first_stab + second_decay, second_stab)
    first_scale = jnp.exp(first_stab + second_decay - stabilizer)
    second_scale = jnp.exp(second_stab - stabilizer)
    matrix_memory = (
        first_memory * first_scale[..., None, None] + second_memory * second_scale[..., None, None]
    )
    normal = first_normal * first_scale[..., None] + second_normal * second_scale[..., None]
    return (matrix_memory, normal, stabilizer, first_decay + second_decay)


def block_output(
    query_matrix,
    key_vectors,
    value_vectors,
    input_gate,
    cumulated,
    prefix_memory,
    prefix_normal,
    prefix_stab,
):
    length = query_matrix.shape[0]
    scaling = 1.0 / math.sqrt(DQK)
    memory_b = prefix_memory.astype(jnp.bfloat16)
    row_index = lax.broadcasted_iota(jnp.int32, (length, length), 0)
    col_index = lax.broadcasted_iota(jnp.int32, (length, length), 1)
    causal = row_index >= col_index

    def block_one_head(head_index, out_buffer):
        head_index = jnp.asarray(head_index).astype(jnp.int32)
        query_rows = lax.dynamic_slice_in_dim(query_matrix, head_index * DQK, DQK, 1)
        key_rows = lax.dynamic_slice_in_dim(key_vectors, head_index * DQK, DQK, 1)
        value_rows = lax.dynamic_slice_in_dim(value_vectors, head_index * DV, DV, 1)
        scores = (
            lax.dot_general(
                query_rows, key_rows, (((1,), (1,)), ((), ())), preferred_element_type=jnp.float32
            )
            * scaling
        )
        cum_head = cumulated[head_index]
        gate_head = input_gate[head_index]
        exponent = jnp.where(
            causal, cum_head[:, None] - cum_head[None, :] + gate_head[None, :], VERY_NEGATIVE
        )
        carried = cum_head + prefix_stab[head_index]
        stabilizer = jnp.maximum(carried, jnp.max(exponent, axis=1))
        weights = jnp.where(causal, jnp.exp(exponent - stabilizer[:, None]) * scores, 0.0)
        factor = jnp.exp(carried - stabilizer)
        carried_term = (
            jnp.dot(query_rows, memory_b[head_index], preferred_element_type=jnp.float32) * scaling
        )
        numerator = factor[:, None] * carried_term + jnp.dot(
            weights.astype(jnp.bfloat16), value_rows, preferred_element_type=jnp.float32
        )
        query_normal = (
            jnp.sum(query_rows.astype(jnp.float32) * prefix_normal[head_index][None, :], axis=1)
            * scaling
        )
        denominator = factor * query_normal + jnp.sum(weights, axis=1)
        result = numerator / jnp.maximum(jnp.abs(denominator), jnp.exp(-stabilizer))[:, None]
        return lax.dynamic_update_slice_in_dim(
            out_buffer, result.astype(jnp.bfloat16), head_index * DV, 1
        )

    return lax.fori_loop(0, H, block_one_head, jnp.zeros((length, H * DV), jnp.bfloat16))


def shards(query_matrix, key_vectors, value_vectors, input_gate, forget_gate):
    log_forget = jax.nn.log_sigmoid(forget_gate)
    cumulated = jnp.cumsum(log_forget, axis=1)
    matrix_memory, normal, stabilizer, decay_sum = summarize(
        key_vectors, value_vectors, input_gate, cumulated
    )
    identity = (
        jnp.zeros_like(matrix_memory),
        jnp.zeros_like(normal),
        jnp.full(stabilizer.shape, VERY_NEGATIVE, jnp.float32),
        jnp.zeros_like(decay_sum),
    )
    prefix = prefix_by_axis((matrix_memory, normal, stabilizer, decay_sum), CTX, combine, identity)
    hidden_state = block_output(
        query_matrix,
        key_vectors,
        value_vectors,
        input_gate,
        cumulated,
        prefix[0],
        prefix[1],
        prefix[2],
    )
    grand_decay = taken_together(decay_sum, CTX)
    post_decay_memory = grand_decay - prefix[3] - decay_sum
    end_stab = stabilizer + post_decay_memory
    final_stabilizer = of_everyone(end_stab, CTX)
    rescale = jnp.exp(end_stab - final_stabilizer)
    final_memory, final_normalizer = (
        lax.psum_scatter(
            matrix_memory * rescale[:, None, None], CTX, scatter_dimension=1, tiled=True
        ),
        lax.psum_scatter(normal * rescale[:, None], CTX, scatter_dimension=1, tiled=True),
    )
    return (hidden_state, final_memory, final_normalizer, final_stabilizer)


def solution(mesh):
    split = Mesh(mesh.devices.reshape(4, 4, mesh.shape["seq"]), ("ctx_0", "ctx_1", "seq"))
    return jax.shard_map(
        shards,
        mesh=split,
        in_specs=(
            P(SEQ_CTX, None),
            P(SEQ_CTX, None),
            P(SEQ_CTX, None),
            P(None, SEQ_CTX),
            P(None, SEQ_CTX),
        ),
        out_specs=(P(SEQ_CTX, None), P("seq", CTX, None), P("seq", CTX), P("seq")),
        check_vma=False,
    )
```

profile of v0, /device:TPU:56, one launch (start us, length us, event | category | flops | bytes accessed | tf_op | source)
XLA Modules:
  0.0 518.9 jit_solution(14754789428189603409)
XLA Ops:
  13.5 65.0 %while.29 = (s32[]{:T(128)}, f32[8,256,512]{2,1,0:T(8,128)}, f32[8,256]{1,0:T(8,128)S(1)}, s32[8]{0:T(128)S(1)}, bf16[1024,2048]{1,0:T(8,128)(2,1)}, /*index=5*/f32[8,1024]{1,0:T(8,128)S(1)}, bf16[1024,4096]{1,0:T(8,128)(2,1)}) while((s32[]{:T(128)}, f32[8,256,512]{2,1,0:T(8,128)}, f32[8,256]{1,0:T(8,128)S(1)}, s32[8]{0:T(128)S(1)}, ...), condition=%wide.region_5.6_spmd.clone, body=%wide.region_3.5_spmd.sunk.clone | while | flops 270008064 | bytes 2641143 | solution.py:73
  18.7 3.0 fusion.122
  26.8 3.0 fusion.122
  34.9 3.0 fusion.122
  43.0 3.0 fusion.122
  51.2 3.0 fusion.122
  59.3 3.0 fusion.122
  67.4 3.0 fusion.122
  75.5 3.0 fusion.122
  79.1 7.8 %all-to-all-start = ((f32[16,1,8]{2,1,0:T(1,128)}), f32[16,1,8]{2,1,0:T(1,128)S(1)}, u32[]{:S(2)}, u32[]{:S(2)}) async-start(f32[16,1,8]{2,1,0:T(1,128)} %broadcast_in_dim.35), calls=%async_computation | async-start | bytes 16384 | tf_op jit(solution)/shard_map/all_to_all | solution.py:42
  88.5 8.6 %all-reduce.3 = (f32[32]{0:T(128)S(1)}, f32[32]{0:T(128)S(1)}) all-reduce(f32[32]{0:T(128)S(1)} %dynamic-update-slice.1, f32[32]{0:T(128)S(1)} %bitcast_dynamic-update-slice_fusion), channel_id=3, replica_groups=mesh['ctx_0'=4,'ctx_1'=4,'seq'=8] {'ctx_1'}, use_global_device_ids=true, to_apply=%add.1 | all-reduce | flops 64 | bytes 512
  97.1 6.7 %all-gather.4 = f32[4,1,8]{2,1,0:T(1,128)S(1)} all-gather(f32[1,1,8]{2,1,0:T(1,128)S(1)} %get-tuple-element.360), channel_id=1, replica_groups=mesh['ctx_0'=4,'ctx_1'=4,'seq'=8] {'ctx_0'}, dimensions={0}, use_global_device_ids=true | all-gather | bytes 160 | tf_op jit(solution)/shard_map/all_gather | solution.py:30
  104.6 8.6 %all-to-all-start.1 = ((f32[16,1,8]{2,1,0:T(1,128)}), f32[16,1,8]{2,1,0:T(1,128)S(1)}, u32[]{:S(2)}, u32[]{:S(2)}) async-start(f32[16,1,8]{2,1,0:T(1,128)} %broadcast_in_dim.36), calls=%async_computation.1 | async-start | bytes 16384 | tf_op jit(solution)/shard_map/all_to_all | solution.py:42
  113.2 6.7 %all-gather.5 = f32[4,1,8]{2,1,0:T(1,128)S(1)} all-gather(f32[1,1,8]{2,1,0:T(1,128)S(1)} %get-tuple-element.359), channel_id=1, replica_groups=mesh['ctx_0'=4,'ctx_1'=4,'seq'=8] {'ctx_0'}, dimensions={0}, use_global_device_ids=true | all-gather | bytes 160 | tf_op jit(solution)/shard_map/all_gather | solution.py:30
  120.3 114.4 %all-gather.11.cloned.1.call-done = f32[32,256,512]{2,1,0:T(8,128)} async-done(((f32[8,256,512]{2,1,0:T(8,128)}), f32[32,256,512]{2,1,0:T(8,128)}) %all-gather.11.cloned.1.call-update) | async-done | bytes 16777232 | tf_op jit(solution)/shard_map/all_gather | solution.py:30
  234.7 8.7 %fusion.38 = f32[1,8,256,512]{3,2,1,0:T(8,128)} fusion(f32[32,256,512]{2,1,0:T(8,128)} %all-gather.11.cloned.1.call-done, f32[8]{0:T(128)S(1)} %get-tuple-element.352, f32[8]{0:T(128)S(1)} %get-tuple-element.353, f32[8]{0:T(128)S(1)} %get-tuple-element.354, f32[8]{0:T(128)S(1)} %get-tuple-element.351, f32[8]{0:T(128)S(1)} %get-tuple-element.355, ...), kind=kLoop, calls=%fused_computation.53 | loop fusion | flops 11534336 | bytes 20971776 | tf_op jit(solution)/shard_map/add | solution.py:84
  245.3 10.8 %all-gather.3 = f32[32,256]{1,0:T(8,128)S(1)} all-gather(f32[8,256]{1,0:T(8,128)S(1)} %get-tuple-element.230), channel_id=5, replica_groups=mesh['ctx_0'=4,'ctx_1'=4,'seq'=8] {'ctx_1'}, dimensions={0}, use_global_device_ids=true | all-gather | bytes 40960 | tf_op jit(solution)/shard_map/all_gather | solution.py:30
  256.2 34.9 %all-reduce.2 = f32[8,256]{1,0:T(8,128)S(1)} all-reduce(f32[8,256]{1,0:T(8,128)S(1)} %broadcast_multiply_fusion.1), channel_id=7, replica_groups=mesh['ctx_0'=4,'ctx_1'=4,'seq'=8] {'ctx_0','ctx_1'}, use_global_device_ids=true, to_apply=%region_14.15.clone | all-reduce | flops 2048 | bytes 16384
  291.2 14.4 %all_gather.47 = f32[4,8,256]{2,1,0:T(8,128)S(1)} all-gather(f32[1,8,256]{2,1,0:T(8,128)S(1)} %fusion.58), channel_id=1, replica_groups=mesh['ctx_0'=4,'ctx_1'=4,'seq'=8] {'ctx_0'}, dimensions={0}, use_global_device_ids=true | all-gather | bytes 40960 | tf_op jit(solution)/shard_map/all_gather | solution.py:30
  306.2 5.1 broadcast_multiply_fusion
  311.4 88.2 %all-gather.9.cloned.1.call-done = f32[4,8,256,512]{3,2,1,0:T(8,128)} async-done(((f32[1,8,256,512]{3,2,1,0:T(8,128)}), f32[4,8,256,512]{3,2,1,0:T(8,128)}) %all-gather.9.cloned.1.call-update) | async-done | bytes 16777232 | tf_op jit(solution)/shard_map/all_gather | solution.py:30
  399.6 15.0 %fusion.31 = bf16[8,256,512]{2,1,0:T(8,128)(2,1)S(1)} fusion(f32[4,8,256,512]{3,2,1,0:T(8,128)} %all-gather.9.cloned.1.call-done, f32[32,256,512]{2,1,0:T(8,128)} %all-gather.11.cloned.1.call-done, f32[8]{0:T(128)S(1)} %get-tuple-element.348, f32[8]{0:T(128)S(1)} %get-tuple-element.357, f32[8]{0:T(128)S(1)} %get-tuple-element.358, ...), kind=kLoop, calls=%fused_computation.42 | loop fusion | flops 37748736 | bytes 35652232 | tf_op jit(solution)/shard_map/convert_element_type | solution.py:102
  414.6 4.4 broadcast_in_dim.34
  419.1 92.4 %while.30 = (s32[]{:T(128)}, bf16[1024,4096]{1,0:T(8,128)(2,1)}, bf16[1024,2048]{1,0:T(8,128)(2,1)}, bf16[8,256,512]{2,1,0:T(8,128)(2,1)S(1)}, f32[8,1024]{1,0:T...) while((s32[]{:T(128)}, bf16[1024,4096]{1,0:T(8,128)(2,1)}, ...), condition=%wide.region_10.11_spmd.clone.clone.clone, body=%wide.region_6.10_spmd.clone.clone.sunk.clone | while | flops 1897669632 | bytes 12947705 | solution.py:143
  (162 shorter events, 117.7 us)
Async XLA Ops:
  8.0 226.7 %all-gather.11.cloned.1.call-start = ((), (), s32[]{:S(2)}) async-start(), calls=%async_computation.5 | async-start | bytes 20971520 | tf_op jit(solution)/shard_map/all_gather | solution.py:30
  78.5 8.4 %copy-start.2 = (u32[128]{0:T(128)S(1)}, u32[128]{0:T(128)}, u32[]{:S(2)}) copy-start(u32[128]{0:T(128)} %constant.130) | copy-start | bytes 1540
  79.1 24.7 %all-to-all-start = ((f32[16,1,8]{2,1,0:T(1,128)}), f32[16,1,8]{2,1,0:T(1,128)S(1)}, u32[]{:S(2)}, u32[]{:S(2)}) async-start(f32[16,1,8]{2,1,0:T(1,128)} %broadcast_in_dim.35), calls=%async_computation | async-start | bytes 16384 | tf_op jit(solution)/shard_map/all_to_all | solution.py:42
  104.6 15.4 %all-to-all-start.1 = ((f32[16,1,8]{2,1,0:T(1,128)}), f32[16,1,8]{2,1,0:T(1,128)S(1)}, u32[]{:S(2)}, u32[]{:S(2)}) async-start(f32[16,1,8]{2,1,0:T(1,128)} %broadcast_in_dim.36), calls=%async_computation.1 | async-start | bytes 16384 | tf_op jit(solution)/shard_map/all_to_all | solution.py:42
  113.2 286.4 %all-gather.9.cloned.1.call-start = ((), (), s32[]{:S(2)}) async-start(), calls=%async_computation.3 | async-start | bytes 20971520 | tf_op jit(solution)/shard_map/all_gather | solution.py:30
  120.0 136.1 %copy-start = (f32[8]{0:T(128)}, f32[8]{0:T(128)S(1)}, u32[]{:S(2)}) copy-start(f32[8]{0:T(128)S(1)} %reduce_max.36) | copy-start | bytes 100
  243.4 0.7 copy-start.1
  243.4 268.0 %reduce-scatter.3.cloned.1.call-start = ((), (), s32[]{:S(2)}) async-start(), calls=%async_computation.4 | async-start | bytes 4456448 | tf_op jit(solution)/shard_map/reduce_scatter | solution.py:175
Sparse Core Ops, SparseCore 0:
  78.7 155.9 all-gather.10
  243.6 156.0 all-gather.8
Sparse Core Ops, SparseCore 1:
  311.4 150.0 reduce-scatter.2
where the time goes:
time: 525 us; the launch traced here: 519 us
  waiting for transfers between devices  203 us (39%)
  blocking collectives  82 us (16%)
  matrix products  81.4 us (16%)
  other arithmetic  68.4 us (13%)
  loops' own time  26.3 us (5%)
  local copies, waits for them, and re-layouts  24.8 us (5%)
  between operations  16.9 us (3%)
  starting transfers between devices  16.5 us (3%)
    all_gather x2, waiting for transfers between devices, prefix_by_axis(): pieces = jax.tree.map(lambda part: lax.all_gather(part, axis), running)  203 us
    unnamed x2, blocking collectives  43.4 us
    all_gather x4, blocking collectives, prefix_by_axis(): pieces = jax.tree.map(lambda part: lax.all_gather(part, axis), running)  38.6 us
    another operation x1, loops' own time, summarize(): lax.map(summarize_one_head, jnp.arange(H, dtype=jnp.int32))  26.1 us
    dot_general x8, matrix products, summarize_one_head(): lax.dot_general(scaled.astype(jnp.bfloat16), value_rows, (((0,), (0,)), (...  23.8 us
    dot_general x8, matrix products, block_one_head(): jnp.dot(weights.astype(jnp.bfloat16), value_rows, preferred_element_type=...  20.2 us
    dot_general x8, matrix products, block_one_head(): jnp.dot(query_rows, memory_b[head_index], preferred_element_type=jnp.floa...  19.9 us
    dot_general x8, matrix products, block_one_head(): lax.dot_general(query_rows, key_rows, (((1,), (1,)), ((), ())), preferred...  17.5 us
  transfers between devices with their start and end apart: 5, of which 2 were waited for; matrix products, arithmetic and copies ran while one was open for 23% of the time, Pallas kernels for 0%

commit v1 on v0

v1 whole, which is shorter than its diff:
```python
import functools

import jax
import jax.numpy as jnp
from jax import lax
from jax.experimental import pallas as pl
from jax.experimental.pallas import tpu as pltpu
from jax.sharding import Mesh
from jax.sharding import PartitionSpec as P

H = 8
DQK = 256
DV = 512
LEN = 1024
NY = 4
NZ = 4
CTX = ("ctx_0", "ctx_1")
SEQ_CTX = ("seq", "ctx_0", "ctx_1")
NEG = -1e30
F32 = jnp.float32
BF16 = jnp.bfloat16
MESH = pl.DeviceIdType.MESH

PATHS = {
    1: (2, 1, 0, 3),
    2: (2, 3, 0, 1),
    3: (3, 2, 1, 0),
    4: (0, 1, 2, 3),
    5: (1, 2, 3, 0),
    6: (1, 0, 3, 2),
}
KINDS = (1, 5, 3, 6, 4, 2, 1, 5)
ZC = {1: (1, 1, 0), 2: (0, 1, 0), 3: (0, 0, 0), 4: (1, 1, 0), 5: (0, 0, 0), 6: (1, 0, 0)}
ZB = {1: (0, 1, 0), 2: (0, 1, 1), 3: (0, 1, 1), 4: (0, 0, 0), 5: (0, 0, 1), 6: (0, 0, 0)}
PO = {1: (0, 0, 0), 2: (0, 0, 0), 3: (0, 0, 1), 4: (1, 0, 0), 5: (1, 0, 1), 6: (1, 0, 1)}
PB_A = {1: 0, 2: 1, 3: 0, 4: 1, 5: 1, 6: 0}
ZA_B = {1: 1, 2: 0, 3: 1, 4: 0, 5: 0, 6: 1}

PIECES = 4
ROWS = DQK // PIECES
UNITS = H * PIECES
LAG_O = 2
LAG_Y = 2
LAG_B = 2
LAG_E = 2
NCOEF = 22
TILE = 256


def pick(h, values):
    out = jnp.int32(values[-1])
    for i in range(len(values) - 1):
        out = jnp.where(h == i, jnp.int32(values[i]), out)
    return out


def kernel(
    q_hbm, k_hbm, v_hbm, gate_ref, forget_ref,
    out_hbm, finm_ref, fins_ref,
    qs, ks, vs, mem, land1, land2, land3, send1, acc, pref,
    cols1, cols2, dens, rows_tmp, arow, rowst, ctab, stats, norms, pnorm, fin,
    in_sem, out_sem, r1, r2, r3, s0, s1, s2, sf, rf, rstat, rnorm, sstat, snorm, loc_sem,
):
    y = lax.axis_index("ctx_0")
    z = lax.axis_index("ctx_1")
    me = y * NZ + z

    def remote(src, dst, ss, rs, yy, zz):
        return pltpu.make_async_remote_copy(
            src_ref=src, dst_ref=dst, send_sem=ss, recv_sem=rs,
            device_id={"ctx_0": yy, "ctx_1": zz}, device_id_type=MESH,
        )

    def load(hbm, dst, h, width, sem):
        return pltpu.make_async_copy(hbm.at[:, h * width:(h + 1) * width], dst.at[h], sem)

    loads = []
    for h in range(H):
        loads.append((
            load(k_hbm, ks, h, DQK, in_sem.at[h]),
            load(v_hbm, vs, h, DV, in_sem.at[H + h]),
            load(q_hbm, qs, h, DQK, in_sem.at[2 * H + h]),
        ))
    for h in range(H):
        loads[h][0].start()
        loads[h][1].start()
    for h in range(H):
        loads[h][2].start()

    barrier = pltpu.get_barrier_semaphore()

    def greet(i, _):
        peer = lax.rem(me + i, NY * NZ)
        pl.semaphore_signal(
            barrier, inc=1,
            device_id={"ctx_0": peer // NZ, "ctx_1": lax.rem(peer, NZ)}, device_id_type=MESH,
        )
        return 0

    lax.fori_loop(1, NY * NZ, greet, 0)

    lane = lax.broadcasted_iota(jnp.int32, (H, LEN), 1)
    f = forget_ref[...]
    cum = jnp.minimum(f, 0.0) - jnp.log1p(jnp.exp(-jnp.abs(f)))
    for s in (1, 2, 4, 8, 16, 32, 64, 128, 256, 512):
        cum = cum + jnp.where(lane >= s, pltpu.roll(cum, s, 1), 0.0)
    a = gate_ref[...] - cum
    b0 = a
    for s in (1, 2, 4, 8, 16, 32, 64, 128, 256, 512):
        b0 = jnp.maximum(b0, jnp.where(lane >= s, pltpu.roll(b0, s, 1), NEG))
    arow[...] = a
    rowst[0] = b0
    rowst[1] = cum
    amax = b0[:, LEN - 1:LEN]
    rows_tmp[...] = jnp.zeros_like(rows_tmp)
    rows_tmp[0:H, :] = jnp.exp(a - amax)
    rows_tmp[H:2 * H, :] = b0
    cols1[...] = rows_tmp[...].T
    decay = cum[:, LEN - 1:LEN]
    stats[me, 0:H] = jnp.broadcast_to(decay + amax, (H, 128))
    stats[me, H:2 * H] = jnp.broadcast_to(decay, (H, 128))
    dens[...] = jnp.zeros_like(dens)

    pl.semaphore_wait(barrier, NY * NZ - 1)

    def spread(table, ss, rs):
        def one(i, _):
            peer = lax.rem(me + i, NY * NZ)
            remote(table.at[me], table.at[me], ss.at[peer], rs.at[me], peer // NZ, lax.rem(peer, NZ)).start()
            return 0
        lax.fori_loop(1, NY * NZ, one, 0)

    def gathered(table, ss, rs):
        def one(i, _):
            peer = lax.rem(me + i, NY * NZ)
            remote(table.at[peer], table.at[peer], ss.at[peer], rs.at[peer], y, z).wait_recv()
            return 0
        lax.fori_loop(1, NY * NZ, one, 0)

    def spread_done(table, ss, rs):
        def one(i, _):
            peer = lax.rem(me + i, NY * NZ)
            remote(table.at[me], table.at[me], ss.at[peer], rs.at[me], y, z).wait_send()
            return 0
        lax.fori_loop(1, NY * NZ, one, 0)

    spread(stats, sstat, rstat)

    def path(h):
        return tuple(pick(h, [PATHS[k][i] for k in KINDS]) for i in range(4))

    def unit(u):
        h = u // PIECES
        c = u - h * PIECES
        return h, c, pl.ds(pl.multiple_of(c * ROWS, ROWS), ROWS)

    def column(table, start, size, h, base):
        x = pltpu.roll(table[pl.ds(start, size), :], lax.rem(128 - h, 128), 1)
        return x[:, base:base + 1]

    def summarize(h, _):
        pltpu.make_async_copy(k_hbm.at[:, 0:DQK], ks.at[h], in_sem.at[h]).wait()
        pltpu.make_async_copy(v_hbm.at[:, 0:DV], vs.at[h], in_sem.at[H + h]).wait()
        scaled = ks[h].astype(F32) * column(cols1, 0, LEN, h, 0)
        norms[me, pl.ds(h, 1), :] = jnp.sum(scaled, axis=0, keepdims=True)
        mem[h] = lax.dot_general(
            scaled.astype(BF16), vs[h], (((0,), (0,)), ((), ())), preferred_element_type=F32
        )
        na, nb, no, nc = path(h)
        for c in range(PIECES):
            u = h * PIECES + c
            rows = pl.ds(c * ROWS, ROWS)

            @pl.when(z == na)
            def _():
                remote(mem.at[h, rows], land1.at[h, rows], s0.at[u], r1.at[u], y, nb).start()

            @pl.when(z == nc)
            def _():
                remote(mem.at[h, rows], land2.at[h, rows], s0.at[u], r2.at[u], y, no).start()
        return 0

    lax.fori_loop(0, H, summarize, 0)
    spread(norms, snorm, rnorm)

    gathered(stats, sstat, rstat)
    sub = lax.broadcasted_iota(jnp.int32, (H, 128), 0)

    def by_head(table):
        out = jnp.zeros((H, 128), F32)
        for h in range(H):
            if table[KINDS[h]] != 0:
                out = jnp.where(sub == h, 1.0, out)
        return out > 0.5

    total = jnp.zeros((H, 128), F32)
    before = jnp.zeros((H, 128), F32)
    top_row = jnp.full((H, 128), NEG, F32)
    top_me = jnp.full((H, 128), NEG, F32)
    top_all = jnp.full((H, 128), NEG, F32)
    logs = []
    for i in range(NY * NZ):
        before = jnp.where(me == i, total, before)
        dec = stats[i, H:2 * H]
        total = total + dec
        w = stats[i, 0:H] - total
        logs.append(w)
        top_row = jnp.maximum(top_row, jnp.where(i < y * NZ, w, NEG))
        top_me = jnp.maximum(top_me, jnp.where(i < me, w, NEG))
        top_all = jnp.maximum(top_all, w)
    here = []
    for j in range(NZ):
        w = logs[j]
        for r in range(1, NY):
            w = jnp.where(y == r, logs[r * NZ + j], w)
        here.append(w)

    def node(i):
        out = here[0]
        for j in range(1, NZ):
            mask = by_head({k: int(PATHS[k][i] == j) for k in PATHS})
            out = jnp.where(mask, here[j], out)
        return out

    l_a, l_b, l_o, l_c = (node(i) for i in range(4))
    l_ab = jnp.maximum(l_a, l_b)
    coefs = [jnp.exp(l_a - l_ab), jnp.exp(l_b - l_ab)]

    def union(base, parts):
        top = base
        for value, mask in parts:
            top = jnp.maximum(top, value if mask is None else jnp.where(mask, value, NEG))
        out = [jnp.exp(base - top)]
        for value, mask in parts:
            e = jnp.exp(value - top)
            out.append(e if mask is None else jnp.where(mask, e, 0.0))
        return top, out

    coefs += union(top_row, [(l_ab, None), (l_o, None), (l_c, None)])[1]
    tops = {}
    for name, table in (("c", ZC), ("b", ZB), ("o", PO)):
        masks = [by_head({k: table[k][i] for k in table}) for i in range(3)]
        tops[name], cs = union(top_row, list(zip((l_ab, l_o, l_c), masks)))
        coefs += cs
    coefs += union(tops["b"], [(l_a, by_head(PB_A))])[1]
    coefs += union(tops["b"], [(l_b, by_head(ZA_B))])[1]
    for i, cf in enumerate(coefs):
        ctab[i] = jnp.concatenate([cf] * (DV // 128), axis=1)

    carried = top_me + before
    prefix_top = carried[:, 0:1]
    b0 = rowst[0]
    cum = rowst[1]
    b = jnp.maximum(prefix_top, b0)
    rows_tmp[0:H, :] = jnp.exp(prefix_top - b) * (1.0 / 16.0)
    rows_tmp[H:2 * H, :] = jnp.exp(b0 - b) * (1.0 / 16.0)
    rows_tmp[2 * H:3 * H, :] = jnp.exp(-(cum + b))
    cols2[...] = rows_tmp[...].T
    fins_ref[H:2 * H, :] = top_all + total

    def normals():
        gathered(norms, snorm, rnorm)
        tot = jnp.zeros((H, DQK), F32)
        mine = jnp.zeros((H, DQK), F32)
        for i in range(NY * NZ):
            n = norms[i]
            w_all = jnp.exp(logs_ref(i) - top_all[:, 0:1])
            w_me = jnp.where(i < me, jnp.exp(logs_ref(i) - top_me[:, 0:1]), 0.0)
            tot = tot + w_all * n
            mine = mine + w_me * n
        pnorm[0:H, :] = mine
        turned = pltpu.roll(tot, lax.rem(DQK - me * (DQK // (NY * NZ)), DQK), 1)
        fins_ref[0:H, :] = turned[:, 0:128]

    def logs_ref(i):
        return logs[i][:, 0:1]

    def coef(i, h):
        return ctab[i, pl.ds(h, 1), :]

    STEP = 16

    def gather_b(u):
        h, c, rows = unit(u)
        na, nb, no, nc = path(h)

        @pl.when(z == nb)
        def _():
            remote(mem.at[h, rows], land1.at[h, rows], s0.at[u], r1.at[u], y, no).wait_recv()
            for t in range(ROWS // STEP):
                part = pl.ds(pl.multiple_of(c * ROWS + t * STEP, STEP), STEP)
                send1[h, part] = coef(0, h) * land1[h, part] + coef(1, h) * mem[h, part]
            remote(send1.at[h, rows], land1.at[h, rows], s0.at[u], r1.at[u], y, no).start()

    def own_o(u):
        h, c, rows = unit(u)
        na, nb, no, nc = path(h)

        @pl.when(z == no)
        def _():
            remote(mem.at[h, rows], land1.at[h, rows], s0.at[u], r1.at[u], y, nb).wait_recv()
            remote(mem.at[h, rows], land2.at[h, rows], s0.at[u], r2.at[u], y, nb).wait_recv()

            @pl.when(y == 0)
            def _():
                land3[h, rows] = jnp.zeros((ROWS, DV), F32)

            @pl.when(y > 0)
            def _():
                remote(mem.at[h, rows], land3.at[h, rows], s0.at[u], r3.at[u], y, nb).wait_recv()

            for t in range(ROWS // STEP):
                part = pl.ds(pl.multiple_of(c * ROWS + t * STEP, STEP), STEP)
                r = land3[h, part]
                xb = land1[h, part]
                xc = land2[h, part]
                mo = mem[h, part]

                def mix(i):
                    return coef(i, h) * r + coef(i + 1, h) * xb + coef(i + 2, h) * mo + coef(i + 3, h) * xc

                send1[h, part] = mix(2)
                land2[h, part] = mix(6)
                land1[h, part] = mix(10)
                pref[h, part] = mix(14).astype(BF16)

            @pl.when(y < NY - 1)
            def _():
                remote(send1.at[h, rows], land3.at[h, rows], s0.at[u], r3.at[u], y + 1, z).start()

            remote(land1.at[h, rows], land3.at[h, rows], s1.at[u], r3.at[u], y, nb).start()
            remote(land2.at[h, rows], land3.at[h, rows], s2.at[u], r3.at[u], y, nc).start()

            @pl.when(y == NY - 1)
            def _():
                for j in range(NZ):
                    part = pl.ds(pl.multiple_of(c * ROWS + j * STEP, STEP), STEP)

                    @pl.when((c != NY - 1) | (z != j))
                    def _():
                        remote(send1.at[h, part], fin.at[h], sf.at[u * NZ + j], rf.at[h], c, j).start()

                    @pl.when((c == NY - 1) & (z == j))
                    def _():
                        fin[h] = send1[h, part]

    def back_b(u):
        h, c, rows = unit(u)
        na, nb, no, nc = path(h)

        @pl.when(z == nb)
        def _():
            remote(mem.at[h, rows], land3.at[h, rows], s0.at[u], r3.at[u], y, no).wait_recv()
            for t in range(ROWS // STEP):
                part = pl.ds(pl.multiple_of(c * ROWS + t * STEP, STEP), STEP)
                zb = land3[h, part]
                pref[h, part] = (coef(18, h) * zb + coef(19, h) * land1[h, part]).astype(BF16)
                land3[h, part] = coef(20, h) * zb + coef(21, h) * mem[h, part]
            remote(land3.at[h, rows], land3.at[h, rows], s1.at[u], r3.at[u], y, na).start()

    def back_e(u):
        h, c, rows = unit(u)
        na, nb, no, nc = path(h)

        @pl.when((z == na) | (z == nc))
        def _():
            remote(mem.at[h, rows], land3.at[h, rows], s0.at[u], r3.at[u], y, nb).wait_recv()
            pref[h, rows] = land3[h, rows].astype(BF16)

    def sends_done(u, _):
        h, c, rows = unit(u)
        na, nb, no, nc = path(h)

        def done(sem):
            remote(mem.at[h, rows], land1.at[h, rows], sem, r1.at[u], y, nb).wait_send()

        @pl.when((z != no) | (y < NY - 1))
        def _():
            done(s0.at[u])

        @pl.when((z == nb) | (z == no))
        def _():
            done(s1.at[u])

        @pl.when(z == no)
        def _():
            done(s2.at[u])

        @pl.when((z == no) & (y == NY - 1))
        def _():
            for j in range(NZ):
                @pl.when((c != NY - 1) | (z != j))
                def _():
                    remote(
                        mem.at[h, pl.ds(0, STEP)], fin.at[h], sf.at[u * NZ + j], rf.at[h], y, nb
                    ).wait_send()
        return 0

    row_id = lax.broadcasted_iota(jnp.int32, (TILE, TILE), 0)
    col_id = lax.broadcasted_iota(jnp.int32, (TILE, TILE), 1)
    lane_id = lax.broadcasted_iota(jnp.int32, (TILE, 128), 1)

    def attend(h, i):
        q = qs[h, i * TILE:(i + 1) * TILE, :]
        bcol = column(cols1, i * TILE, TILE, h, H)
        total = jnp.zeros((TILE, DV), F32)
        den = jnp.zeros((TILE, 1), F32)
        for j in range(i + 1):
            span = slice(j * TILE, (j + 1) * TILE)
            s = lax.dot_general(q, ks[h, span, :], (((1,), (1,)), ((), ())), preferred_element_type=F32)
            p = jnp.exp(arow[pl.ds(h, 1), span] - bcol) * s
            if j == i:
                p = jnp.where(row_id >= col_id, p, 0.0)
            den = den + jnp.sum(p, axis=1, keepdims=True)
            total = total + jnp.dot(p.astype(BF16), vs[h, span, :], preferred_element_type=F32)
        acc[h, i * TILE:(i + 1) * TILE, :] = total
        at = slice(i * TILE, (i + 1) * TILE)
        dens[at, :] = jnp.where(lane_id == h, den, dens[at, :])

    def finish(h):
        def tile(i, _):
            at = pl.ds(pl.multiple_of(i * TILE, TILE), TILE)
            q = qs[h, at, :]
            carried_term = jnp.dot(q, pref[h], preferred_element_type=F32)
            qn = jnp.sum(q.astype(F32) * pnorm[pl.ds(h, 1), :], axis=1, keepdims=True)
            start = pl.multiple_of(i * TILE, TILE)
            w1 = column(cols2, start, TILE, h, 0)
            w2 = column(cols2, start, TILE, h, H)
            floor = column(cols2, start, TILE, h, 2 * H)
            den = column(dens, start, TILE, h, 0)
            bottom = jnp.maximum(jnp.abs(w1 * qn + w2 * den), floor)
            vs[h, at, :] = ((w1 * carried_term + w2 * acc[h, at, :]) / bottom).astype(BF16)
            return 0

        lax.fori_loop(0, LEN // TILE, tile, 0)
        pltpu.make_async_copy(
            vs.at[h], out_hbm.at[:, pl.ds(pl.multiple_of(h * DV, DV), DV)], out_sem.at[h]
        ).start()

    lag_o = LAG_O + LAG_Y * y
    lag_b = lag_o + LAG_B
    lag_e = lag_b + LAG_E

    def guarded(fn, u):
        @pl.when((u >= 0) & (u < UNITS))
        def _():
            fn(jnp.clip(u, 0, UNITS - 1))

    normals()

    def main(hh, _):
        for c in range(PIECES):
            v = hh * PIECES + c
            guarded(gather_b, v)
            guarded(own_o, v - lag_o)
            guarded(back_b, v - lag_b)
            guarded(back_e, v - lag_e)

            @pl.when(hh < H)
            def _():
                h = jnp.minimum(hh, H - 1)
                if c == 0:
                    pltpu.make_async_copy(q_hbm.at[:, 0:DQK], qs.at[h], in_sem.at[2 * H + h]).wait()
                attend(h, c)
        hf = hh - (lag_e + PIECES - 1) // PIECES

        @pl.when((hf >= 0) & (hf < H))
        def _():
            finish(jnp.clip(hf, 0, H - 1))
        return 0

    max_lag = LAG_O + LAG_Y * (NY - 1) + LAG_B + LAG_E
    lax.fori_loop(0, H + (max_lag + PIECES - 1) // PIECES, main, 0)

    def last(h, _):
        na, nb, no, nc = path(h)

        @pl.when((y != NY - 1) | (z != no))
        def _():
            remote(mem.at[h, pl.ds(0, STEP)], fin.at[h], s0.at[0], rf.at[h], y, nb).wait_recv()
        finm_ref[h] = fin[h]
        pltpu.make_async_copy(vs.at[h], out_hbm.at[:, 0:DV], out_sem.at[h]).wait()
        return 0

    lax.fori_loop(0, H, last, 0)
    lax.fori_loop(0, UNITS, sends_done, 0)
    spread_done(stats, sstat, rstat)
    spread_done(norms, snorm, rnorm)


def shards(query_matrix, key_vectors, value_vectors, input_gate, forget_gate):
    vmem = pl.BlockSpec(memory_space=pltpu.VMEM)
    hbm = pl.BlockSpec(memory_space=pl.ANY)
    dma = pltpu.SemaphoreType.DMA
    ctx = NY * NZ
    hidden, final_memory, small = pl.pallas_call(
        kernel,
        out_shape=(
            jax.ShapeDtypeStruct((LEN, H * DV), BF16),
            jax.ShapeDtypeStruct((H, DQK // ctx, DV), F32),
            jax.ShapeDtypeStruct((2 * H, 128), F32),
        ),
        in_specs=[hbm, hbm, hbm, vmem, vmem],
        out_specs=(hbm, vmem, vmem),
        scratch_shapes=[
            pltpu.VMEM((H, LEN, DQK), BF16),
            pltpu.VMEM((H, LEN, DQK), BF16),
            pltpu.VMEM((H, LEN, DV), BF16),
            pltpu.VMEM((H, DQK, DV), F32),
            pltpu.VMEM((H, DQK, DV), F32),
            pltpu.VMEM((H, DQK, DV), F32),
            pltpu.VMEM((H, DQK, DV), F32),
            pltpu.VMEM((H, DQK, DV), F32),
            pltpu.VMEM((H, LEN, DV), F32),
            pltpu.VMEM((H, DQK, DV), BF16),
            pltpu.VMEM((LEN, 128), F32),
            pltpu.VMEM((LEN, 128), F32),
            pltpu.VMEM((LEN, 128), F32),
            pltpu.VMEM((128, LEN), F32),
            pltpu.VMEM((H, LEN), F32),
            pltpu.VMEM((2, H, LEN), F32),
            pltpu.VMEM((NCOEF, H, DV), F32),
            pltpu.VMEM((ctx, 2 * H, 128), F32),
            pltpu.VMEM((ctx, H, DQK), F32),
            pltpu.VMEM((H, DQK), F32),
            pltpu.VMEM((H, DQK // ctx, DV), F32),
            dma((3 * H,)),
            dma((H,)),
            dma((UNITS,)),
            dma((UNITS,)),
            dma((UNITS,)),
            dma((UNITS,)),
            dma((UNITS,)),
            dma((UNITS,)),
            dma((UNITS * NZ,)),
            dma((H,)),
            dma((ctx,)),
            dma((ctx,)),
            dma((ctx,)),
            dma((ctx,)),
            dma((1,)),
        ],
        compiler_params=pltpu.CompilerParams(
            collective_id=0, has_side_effects=True, vmem_limit_bytes=67_000_000
        ),
        name="mlstm_cell",
    )(query_matrix, key_vectors, value_vectors, input_gate, forget_gate)
    return (hidden, final_memory, small[0:H, 0:DQK // ctx], small[H:2 * H, 0])


def solution(mesh):
    split = Mesh(mesh.devices.reshape(NY, NZ, mesh.shape["seq"]), ("ctx_0", "ctx_1", "seq"))
    return jax.shard_map(
        shards,
        mesh=split,
        in_specs=(
            P(SEQ_CTX, None),
            P(SEQ_CTX, None),
            P(SEQ_CTX, None),
            P(None, SEQ_CTX),
            P(None, SEQ_CTX),
        ),
        out_specs=(P(SEQ_CTX, None), P("seq", CTX, None), P("seq", CTX), P("seq")),
        check_vma=False,
    )
```

time: 525 us -> 165 us (0.31); the launches traced: 519 us -> 164 us
  waiting for transfers between devices: 203 us -> 0 us
  Pallas kernels: 0 us -> 153 us
  blocking collectives: 82 us -> 0 us
  matrix products: 81.4 us -> 0 us
  other arithmetic: 68.4 us -> 0 us
  loops' own time: 26.3 us -> 0 us
  starting transfers between devices: 16.5 us -> 0 us
  between operations: 16.9 us -> 0.64 us
  local copies, waits for them, and re-layouts: 24.8 us -> 11.2 us
    all_gather x2 -> x0, waiting for transfers between devices: 203 us -> none  [prefix_by_axis(): pieces = jax.tree.map(lambda part: lax.all_gather(part, axis), running)]
    pallas_call x0 -> x1, Pallas kernels: none -> 153 us  [shards(): pl.pallas_call(kernel, out_shape=(jax.ShapeDtypeStruct((LEN, H * DV), BF1...]
    dot_general x32 -> x0, matrix products: 81.4 us -> none  [the longest x8 23.8 us: summarize_one_head(): lax.dot_general(scaled.astype(jnp.bfloat16), value_rows, (((0,), (0,)), (...]
    unnamed x2 -> x0, blocking collectives: 43.4 us -> none
    all_gather x4 -> x0, blocking collectives: 38.6 us -> none  [prefix_by_axis(): pieces = jax.tree.map(lambda part: lax.all_gather(part, axis), running)]
    another operation x2 -> x0, loops' own time: 26.3 us -> none  [the longest x1 26.1 us: summarize(): lax.map(summarize_one_head, jnp.arange(H, dtype=jnp.int32))]
    reduce_sum x17 -> x0, other arithmetic: 20.2 us -> none  [the longest x8 10.1 us: summarize_one_head(): return (matrix_memory, jnp.sum(scaled, axis=0))]
    all_to_all x2 -> x0, starting transfers between devices: 16.4 us -> none  [copy_for_each(): lax.all_to_all(jnp.broadcast_to(x[None], (size, *x.shape)), axis, 0, 0, t...]
  transfers between devices with their start and end apart: 5 -> 0, of which waited for: 2 -> 0; matrix products, arithmetic and copies ran while one was open for 23% -> 0% of each run, Pallas kernels for 0% -> 0%
where the time goes in v1:
time: 165 us; the launch traced here: 164 us
  Pallas kernels  153 us (93%)
  local copies, waits for them, and re-layouts  11.2 us (7%)
    pallas_call x1, Pallas kernels, shards(): pl.pallas_call(kernel, out_shape=(jax.ShapeDtypeStruct((LEN, H * DV), BF1...  153 us
    unnamed x4, local copies, waits for them, and re-layouts  8.64 us

profile of v1, /device:TPU:56, one launch (start us, length us, event | category | flops | bytes accessed | tf_op | source)
XLA Modules:
  0.0 164.4 jit_solution(17780068375056372754)
XLA Ops:
  0.6 152.5 %mlstm_cell.1 = (bf16[1024,4096]{1,0:T(8,128)(2,1)}, f32[8,16,512]{2,1,0:T(8,128)}, f32[16,128]{1,0:T(8,128)}) custom-call(bf16[1024,2048]{1,0:T(8,128)(2,1)} %q_hbm.1, bf16[1024,2048]{1,0:T(8,128)(2,1)} %k_hbm.1, bf16[1024,4096]{1,0:T(8,128)(2,1)} %v_hbm.1, f32[8,1024]{1,0:T(8,128)} %gate_ref.1, f32[8,1024]{1,0:T(8,128)} %forget_ref.1), custom_call_target="tpu_custom_call" | custom-call | tf_op jit(solution)/shard_map/mlstm_cell/pallas_call | solution.py:496
  153.2 1.3 slice.6
  154.5 1.3 slice_reduce_fusion
  155.8 0.0 copy-start
  155.8 7.9 %copy.11 = bf16[1024,4096]{1,0:T(8,128)(2,1)} copy(bf16[1024,4096]{1,0:T(8,128)(2,1)} %get-tuple-element.14) | data formatting | bytes 16777216
  163.7 0.0 copy-done
  163.7 0.7 copy.12
Async XLA Ops:
  155.8 7.9 %copy-start = (f32[8,16,512]{2,1,0:T(8,128)S(1)}, f32[8,16,512]{2,1,0:T(8,128)}, u32[]{:S(2)}) copy-start(f32[8,16,512]{2,1,0:T(8,128)} %get-tuple-element.15) | copy-start | bytes 786436

commit v2 on v1

--- a/solution.py
+++ b/solution.py
@@ -29,7 +29,7 @@
     5: (1, 2, 3, 0),
     6: (1, 0, 3, 2),
 }
-KINDS = (1, 5, 3, 6, 4, 2, 1, 5)
+KINDS = (2, 5, 1, 3, 5, 4, 1, 6)
 ZC = {1: (1, 1, 0), 2: (0, 1, 0), 3: (0, 0, 0), 4: (1, 1, 0), 5: (0, 0, 0), 6: (1, 0, 0)}
 ZB = {1: (0, 1, 0), 2: (0, 1, 1), 3: (0, 1, 1), 4: (0, 0, 0), 5: (0, 0, 1), 6: (0, 0, 0)}
 PO = {1: (0, 0, 0), 2: (0, 0, 0), 3: (0, 0, 1), 4: (1, 0, 0), 5: (1, 0, 1), 6: (1, 0, 1)}
@@ -39,10 +39,13 @@
 PIECES = 4
 ROWS = DQK // PIECES
 UNITS = H * PIECES
-LAG_O = 2
-LAG_Y = 2
-LAG_B = 2
-LAG_E = 2
+LAG_O = 15
+LAG_Y = 4
+LAG_B = 12
+LAG_E = 9
+LAG_A = 0
+LEAD = 17
+EARLY = 8
 NCOEF = 22
 TILE = 256
 
@@ -166,22 +169,29 @@
         mem[h] = lax.dot_general(
             scaled.astype(BF16), vs[h], (((0,), (0,)), ((), ())), preferred_element_type=F32
         )
-        na, nb, no, nc = path(h)
+        return 0
+
+    def first_send(u):
+        h, c, rows = unit(u)
+        na, nb, no, nc = path(h)
+
+        @pl.when(z == na)
+        def _():
+            remote(mem.at[h, rows], land1.at[h, rows], s0.at[u], r1.at[u], y, nb).start()
+
+        @pl.when(z == nc)
+        def _():
+            remote(mem.at[h, rows], land2.at[h, rows], s0.at[u], r2.at[u], y, no).start()
+
+    def begin(h, _):
+        summarize(h, 0)
         for c in range(PIECES):
-            u = h * PIECES + c
-            rows = pl.ds(c * ROWS, ROWS)
-
-            @pl.when(z == na)
+            @pl.when(h * PIECES + c < LEAD)
             def _():
-                remote(mem.at[h, rows], land1.at[h, rows], s0.at[u], r1.at[u], y, nb).start()
-
-            @pl.when(z == nc)
-            def _():
-                remote(mem.at[h, rows], land2.at[h, rows], s0.at[u], r2.at[u], y, no).start()
+                first_send(h * PIECES + c)
         return 0
 
-    lax.fori_loop(0, H, summarize, 0)
-    spread(norms, snorm, rnorm)
+    lax.fori_loop(0, EARLY, begin, 0)
 
     gathered(stats, sstat, rstat)
     sub = lax.broadcasted_iota(jnp.int32, (H, 128), 0)
@@ -446,23 +456,34 @@
         def _():
             fn(jnp.clip(u, 0, UNITS - 1))
 
-    normals()
-
     def main(hh, _):
+        @pl.when(hh + EARLY < H)
+        def _():
+            summarize(jnp.minimum(hh + EARLY, H - 1), 0)
+
+        @pl.when(hh == H - EARLY)
+        def _():
+            spread(norms, snorm, rnorm)
+
+        @pl.when(hh == H - EARLY + 1)
+        def _():
+            normals()
+
         for c in range(PIECES):
             v = hh * PIECES + c
+            guarded(first_send, v + LEAD)
             guarded(gather_b, v)
             guarded(own_o, v - lag_o)
             guarded(back_b, v - lag_b)
             guarded(back_e, v - lag_e)
 
-            @pl.when(hh < H)
+            @pl.when((hh >= LAG_A) & (hh < H + LAG_A))
             def _():
-                h = jnp.minimum(hh, H - 1)
+                h = jnp.clip(hh - LAG_A, 0, H - 1)
                 if c == 0:
                     pltpu.make_async_copy(q_hbm.at[:, 0:DQK], qs.at[h], in_sem.at[2 * H + h]).wait()
                 attend(h, c)
-        hf = hh - (lag_e + PIECES - 1) // PIECES
+        hf = hh - jnp.maximum((lag_e + PIECES - 1) // PIECES, max(H - EARLY + 1, LAG_A))
 
         @pl.when((hf >= 0) & (hf < H))
         def _():
@@ -470,7 +491,7 @@
         return 0
 
     max_lag = LAG_O + LAG_Y * (NY - 1) + LAG_B + LAG_E
-    lax.fori_loop(0, H + (max_lag + PIECES - 1) // PIECES, main, 0)
+    lax.fori_loop(0, H + max((max_lag + PIECES - 1) // PIECES, H - EARLY + 1, LAG_A), main, 0)
 
     def last(h, _):
         na, nb, no, nc = path(h)

time: 165 us -> 121 us (0.73)
  Pallas kernels: 153 us -> 109 us
    pallas_call x1, Pallas kernels: 153 us -> 109 us  [shards(): pl.pallas_call(kernel, out_shape=(jax.ShapeDtypeStruct((LEN, H * DV), BF1...]
where the time goes in v2:
time: 121 us
  Pallas kernels  109 us (90%)
  local copies, waits for them, and re-layouts  11.2 us (9%)
    pallas_call x1, Pallas kernels, shards(): pl.pallas_call(kernel, out_shape=(jax.ShapeDtypeStruct((LEN, H * DV), BF1...  109 us
    unnamed x4, local copies, waits for them, and re-layouts  8.64 us
    slice x2, local copies, waits for them, and re-layouts, shards(): return (hidden, final_memory, small[0:H, 0:DQK // ctx], small[H:2 * H, 0])  2.58 us

profile of v2, /device:TPU:56, one launch (start us, length us, event | category | flops | bytes accessed | tf_op | source)
XLA Modules:
  0.0 120.6 jit_solution(9443367427355210004)
XLA Ops:
  0.6 108.8 %mlstm_cell.1 = (bf16[1024,4096]{1,0:T(8,128)(2,1)}, f32[8,16,512]{2,1,0:T(8,128)}, f32[16,128]{1,0:T(8,128)}) custom-call(bf16[1024,2048]{1,0:T(8,128)(2,1)} %q_hbm.1, bf16[1024,2048]{1,0:T(8,128)(2,1)} %k_hbm.1, bf16[1024,4096]{1,0:T(8,128)(2,1)} %v_hbm.1, f32[8,1024]{1,0:T(8,128)} %gate_ref.1, f32[8,1024]{1,0:T(8,128)} %forget_ref.1), custom_call_target="tpu_custom_call" | custom-call | tf_op jit(solution)/shard_map/mlstm_cell/pallas_call | solution.py:517
  109.4 1.3 %slice.6 = f32[8,16]{1,0:T(8,128)} slice(f32[16,128]{1,0:T(8,128)} %get-tuple-element.9), slice={[0:8], [0:16]} | slice | bytes 1024 | tf_op jit(solution)/shard_map/slice | solution.py:569
  110.7 1.3 %slice_reduce_fusion = f32[8]{0:T(128)} fusion(f32[16,128]{1,0:T(8,128)} %get-tuple-element.9), kind=kLoop, calls=%fused_computation | loop fusion | bytes 64 | tf_op jit(solution)/shard_map/slice | solution.py:569
  112.0 0.0 copy-start
  112.0 7.9 %copy.11 = bf16[1024,4096]{1,0:T(8,128)(2,1)} copy(bf16[1024,4096]{1,0:T(8,128)(2,1)} %get-tuple-element.14) | data formatting | bytes 16777216
  119.9 0.0 copy-done
  119.9 0.7 copy.12
Async XLA Ops:
  112.0 7.9 %copy-start = (f32[8,16,512]{2,1,0:T(8,128)S(1)}, f32[8,16,512]{2,1,0:T(8,128)}, u32[]{:S(2)}) copy-start(f32[8,16,512]{2,1,0:T(8,128)} %get-tuple-element.15) | copy-start | bytes 786436

commit v3 on v2

--- a/solution.py
+++ b/solution.py
@@ -59,10 +59,10 @@
 
 def kernel(
     q_hbm, k_hbm, v_hbm, gate_ref, forget_ref,
-    out_hbm, finm_ref, fins_ref,
-    qs, ks, vs, mem, land1, land2, land3, send1, acc, pref,
+    vs, finm_ref, fins_ref,
+    qs, ks, mem, land1, land2, land3, send1, acc, pref,
     cols1, cols2, dens, rows_tmp, arow, rowst, ctab, stats, norms, pnorm, fin,
-    in_sem, out_sem, r1, r2, r3, s0, s1, s2, sf, rf, rstat, rnorm, sstat, snorm, loc_sem,
+    in_sem, r1, r2, r3, s0, s1, s2, sf, rf, rstat, rnorm, sstat, snorm, loc_sem,
 ):
     y = lax.axis_index("ctx_0")
     z = lax.axis_index("ctx_1")
@@ -443,9 +443,6 @@
             return 0
 
         lax.fori_loop(0, LEN // TILE, tile, 0)
-        pltpu.make_async_copy(
-            vs.at[h], out_hbm.at[:, pl.ds(pl.multiple_of(h * DV, DV), DV)], out_sem.at[h]
-        ).start()
 
     lag_o = LAG_O + LAG_Y * y
     lag_b = lag_o + LAG_B
@@ -464,10 +461,6 @@
         @pl.when(hh == H - EARLY)
         def _():
             spread(norms, snorm, rnorm)
-
-        @pl.when(hh == H - EARLY + 1)
-        def _():
-            normals()
 
         for c in range(PIECES):
             v = hh * PIECES + c
@@ -485,6 +478,10 @@
                 attend(h, c)
         hf = hh - jnp.maximum((lag_e + PIECES - 1) // PIECES, max(H - EARLY + 1, LAG_A))
 
+        @pl.when(hf == 0)
+        def _():
+            normals()
+
         @pl.when((hf >= 0) & (hf < H))
         def _():
             finish(jnp.clip(hf, 0, H - 1))
@@ -500,13 +497,26 @@
         def _():
             remote(mem.at[h, pl.ds(0, STEP)], fin.at[h], s0.at[0], rf.at[h], y, nb).wait_recv()
         finm_ref[h] = fin[h]
-        pltpu.make_async_copy(vs.at[h], out_hbm.at[:, 0:DV], out_sem.at[h]).wait()
         return 0
 
     lax.fori_loop(0, H, last, 0)
     lax.fori_loop(0, UNITS, sends_done, 0)
     spread_done(stats, sstat, rstat)
     spread_done(norms, snorm, rnorm)
+
+
+def write_out(heads, finm, fins, out_hbm, finm_hbm, norm_ref, stab_ref, sem):
+    copies = [
+        pltpu.make_async_copy(heads.at[h], out_hbm.at[:, h * DV:(h + 1) * DV], sem.at[h])
+        for h in range(H)
+    ]
+    copies.append(pltpu.make_async_copy(finm, finm_hbm, sem.at[H]))
+    for copy in copies:
+        copy.start()
+    norm_ref[...] = fins[0:H, 0:DQK // (NY * NZ)]
+    stab_ref[...] = fins[H:2 * H, 0:1].reshape(H)
+    for copy in copies:
+        copy.wait()
 
 
 def shards(query_matrix, key_vectors, value_vectors, input_gate, forget_gate):
@@ -514,19 +524,18 @@
     hbm = pl.BlockSpec(memory_space=pl.ANY)
     dma = pltpu.SemaphoreType.DMA
     ctx = NY * NZ
-    hidden, final_memory, small = pl.pallas_call(
+    heads, final_memory, small = pl.pallas_call(
         kernel,
         out_shape=(
-            jax.ShapeDtypeStruct((LEN, H * DV), BF16),
-            jax.ShapeDtypeStruct((H, DQK // ctx, DV), F32),
-            jax.ShapeDtypeStruct((2 * H, 128), F32),
+            pltpu.VMEM((H, LEN, DV), BF16),
+            pltpu.VMEM((H, DQK // ctx, DV), F32),
+            pltpu.VMEM((2 * H, 128), F32),
         ),
         in_specs=[hbm, hbm, hbm, vmem, vmem],
-        out_specs=(hbm, vmem, vmem),
+        out_specs=(vmem, vmem, vmem),
         scratch_shapes=[
             pltpu.VMEM((H, LEN, DQK), BF16),
             pltpu.VMEM((H, LEN, DQK), BF16),
-            pltpu.VMEM((H, LEN, DV), BF16),
             pltpu.VMEM((H, DQK, DV), F32),
             pltpu.VMEM((H, DQK, DV), F32),
             pltpu.VMEM((H, DQK, DV), F32),
@@ -546,7 +555,6 @@
             pltpu.VMEM((H, DQK), F32),
             pltpu.VMEM((H, DQK // ctx, DV), F32),
             dma((3 * H,)),
-            dma((H,)),
             dma((UNITS,)),
             dma((UNITS,)),
             dma((UNITS,)),
@@ -562,11 +570,24 @@
             dma((1,)),
         ],
         compiler_params=pltpu.CompilerParams(
-            collective_id=0, has_side_effects=True, vmem_limit_bytes=67_000_000
+            collective_id=0, has_side_effects=True, vmem_limit_bytes=57_000_000
         ),
         name="mlstm_cell",
     )(query_matrix, key_vectors, value_vectors, input_gate, forget_gate)
-    return (hidden, final_memory, small[0:H, 0:DQK // ctx], small[H:2 * H, 0])
+    return pl.pallas_call(
+        write_out,
+        out_shape=(
+            jax.ShapeDtypeStruct((LEN, H * DV), BF16),
+            jax.ShapeDtypeStruct((H, DQK // ctx, DV), F32),
+            jax.ShapeDtypeStruct((H, DQK // ctx), F32),
+            jax.ShapeDtypeStruct((H,), F32),
+        ),
+        in_specs=[hbm, hbm, vmem],
+        out_specs=(hbm, hbm, vmem, vmem),
+        scratch_shapes=[dma((H + 1,))],
+        compiler_params=pltpu.CompilerParams(vmem_limit_bytes=1_000_000),
+        name="write_out",
+    )(heads, final_memory, small)
 
 
 def solution(mesh):

time: 121 us -> 108 us (0.89)
  local copies, waits for them, and re-layouts: 11.2 us -> 0 us
  Pallas kernels: 109 us -> 107 us
    unnamed x4 -> x0, local copies, waits for them, and re-layouts: 8.64 us -> none
    slice x2 -> x0, local copies, waits for them, and re-layouts: 2.58 us -> none  [shards(): return (hidden, final_memory, small[0:H, 0:DQK // ctx], small[H:2 * H, 0])]
    pallas_call x1 -> x2, Pallas kernels: 109 us -> 107 us  [the longest x1 103 us: shards(): pl.pallas_call(kernel, out_shape=(pltpu.VMEM((H, LEN, DV), BF16), pltpu.V...]
where the time goes in v3:
time: 108 us
  Pallas kernels  107 us (99%)
    pallas_call x1, Pallas kernels, shards(): pl.pallas_call(kernel, out_shape=(pltpu.VMEM((H, LEN, DV), BF16), pltpu.V...  103 us
    pallas_call x1, Pallas kernels, shards(): pl.pallas_call(write_out, out_shape=(jax.ShapeDtypeStruct((LEN, H * DV),...  4.02 us

profile of v3, /device:TPU:56, one launch (start us, length us, event | category | flops | bytes accessed | tf_op | source)
XLA Modules:
  0.0 107.7 jit_solution(7706411249226096745)
XLA Ops:
  0.6 103.1 %mlstm_cell.1 = (bf16[8,1024,512]{2,1,0:T(8,128)(2,1)S(1)}, f32[8,16,512]{2,1,0:T(8,128)S(1)}, f32[16,128]{1,0:T(8,128)S(1)}) custom-call(bf16[1024,2048]{1,0:T(8,128)(2,1)} %q_hbm.1, bf16[1024,2048]{1,0:T(8,128)(2,1)} %k_hbm.1, bf16[1024,4096]{1,0:T(8,128)(2,1)} %v_hbm.1, f32[8,1024]{1,0:T(8,128)} %gate_ref.1, f32[8,1024]{1,0:T(8,128)} %forget_ref.1), custom_call_target="tpu_custom_call" | custom-call | tf_op jit(solution)/shard_map/mlstm_cell/pallas_call | solution.py:527
  103.7 4.0 %write_out.1 = (bf16[1024,4096]{1,0:T(8,128)(2,1)}, f32[8,16,512]{2,1,0:T(8,128)}, f32[8,16]{1,0:T(8,128)}, f32[8]{0:T(128)}) custom-call(bf16[8,1024,512]{2,1,0:T(8,128)(2,1)S(1)} %get-tuple-element.7.heads, f32[8,16,512]{2,1,0:T(8,128)S(1)} %get-tuple-element.8.finm, f32[16,128]{1,0:T(8,128)S(1)} %get-tuple-element.9.fins), custom_call_target="tpu_custom_call" | custom-call | tf_op jit(solution)/shard_map/write_out/pallas_call | solution.py:577

commit v4 on v3

--- a/solution.py
+++ b/solution.py
@@ -39,30 +39,27 @@
 PIECES = 4
 ROWS = DQK // PIECES
 UNITS = H * PIECES
+STEP = DQK // (NY * NZ)
+SHARES = ROWS // STEP
+TILES = 4
+EACH = PIECES // TILES
 LAG_O = 15
 LAG_Y = 4
 LAG_B = 12
 LAG_E = 9
-LAG_A = 0
+LAG_A = 1
 LEAD = 17
 EARLY = 8
 NCOEF = 22
 TILE = 256
 
 
-def pick(h, values):
-    out = jnp.int32(values[-1])
-    for i in range(len(values) - 1):
-        out = jnp.where(h == i, jnp.int32(values[i]), out)
-    return out
-
-
 def kernel(
-    q_hbm, k_hbm, v_hbm, gate_ref, forget_ref,
+    q_hbm, k_hbm, v_hbm, gate_hbm, forget_hbm,
     vs, finm_ref, fins_ref,
     qs, ks, mem, land1, land2, land3, send1, acc, pref,
-    cols1, cols2, dens, rows_tmp, arow, rowst, ctab, stats, norms, pnorm, fin,
-    in_sem, r1, r2, r3, s0, s1, s2, sf, rf, rstat, rnorm, sstat, snorm, loc_sem,
+    gate_ref, forget_ref, cols1, cols2, dens, rows_tmp, arow, rowst, ctab, stats, norms, pnorm, fin,
+    in_sem, r1, r2, r3, s0, s1, s2, sf, rf, rstat, rnorm, sstat, snorm, gate_sem,
 ):
     y = lax.axis_index("ctx_0")
     z = lax.axis_index("ctx_1")
@@ -77,6 +74,23 @@
     def load(hbm, dst, h, width, sem):
         return pltpu.make_async_copy(hbm.at[:, h * width:(h + 1) * width], dst.at[h], sem)
 
+    barrier = pltpu.get_barrier_semaphore()
+
+    def greet(i, _):
+        peer = lax.rem(me + i, NY * NZ)
+        pl.semaphore_signal(
+            barrier, inc=1,
+            device_id={"ctx_0": peer // NZ, "ctx_1": lax.rem(peer, NZ)}, device_id_type=MESH,
+        )
+        return 0
+
+    gates = (
+        pltpu.make_async_copy(gate_hbm, gate_ref, gate_sem.at[0]),
+        pltpu.make_async_copy(forget_hbm, forget_ref, gate_sem.at[1]),
+    )
+    gates[1].start()
+    gates[0].start()
+    lax.fori_loop(1, NY * NZ, greet, 0)
     loads = []
     for h in range(H):
         loads.append((
@@ -90,17 +104,8 @@
     for h in range(H):
         loads[h][2].start()
 
-    barrier = pltpu.get_barrier_semaphore()
-
-    def greet(i, _):
-        peer = lax.rem(me + i, NY * NZ)
-        pl.semaphore_signal(
-            barrier, inc=1,
-            device_id={"ctx_0": peer // NZ, "ctx_1": lax.rem(peer, NZ)}, device_id_type=MESH,
-        )
-        return 0
-
-    lax.fori_loop(1, NY * NZ, greet, 0)
+    gates[0].wait()
+    gates[1].wait()
 
     lane = lax.broadcasted_iota(jnp.int32, (H, LEN), 1)
     f = forget_ref[...]
@@ -149,12 +154,24 @@
 
     spread(stats, sstat, rstat)
 
-    def path(h):
-        return tuple(pick(h, [PATHS[k][i] for k in KINDS]) for i in range(4))
+    roles = jnp.int32(0)
+    for r in range(NZ):
+        code = sum(PATHS[k].index(r) << (2 * h) for h, k in enumerate(KINDS))
+        roles = jnp.where(z == r, jnp.int32(code), roles)
+    steps = sum(((PATHS[k][1] - PATHS[k][0]) % NZ) << (2 * h) for h, k in enumerate(KINDS))
+
+    def role(h):
+        return jnp.right_shift(roles, 2 * h) & 3
+
+    def along(h):
+        return (z + (jnp.right_shift(jnp.int32(steps), 2 * h) & 3)) & 3
+
+    def against(h):
+        return (z + 4 - (jnp.right_shift(jnp.int32(steps), 2 * h) & 3)) & 3
 
     def unit(u):
-        h = u // PIECES
-        c = u - h * PIECES
+        h = jnp.right_shift(u, PIECES.bit_length() - 1)
+        c = u & (PIECES - 1)
         return h, c, pl.ds(pl.multiple_of(c * ROWS, ROWS), ROWS)
 
     def column(table, start, size, h, base):
@@ -173,15 +190,15 @@
 
     def first_send(u):
         h, c, rows = unit(u)
-        na, nb, no, nc = path(h)
-
-        @pl.when(z == na)
-        def _():
-            remote(mem.at[h, rows], land1.at[h, rows], s0.at[u], r1.at[u], y, nb).start()
-
-        @pl.when(z == nc)
-        def _():
-            remote(mem.at[h, rows], land2.at[h, rows], s0.at[u], r2.at[u], y, no).start()
+        part = role(h)
+
+        @pl.when(part == 0)
+        def _():
+            remote(mem.at[h, rows], land1.at[h, rows], s0.at[u], r1.at[u], y, along(h)).start()
+
+        @pl.when(part == 3)
+        def _():
+            remote(mem.at[h, rows], land2.at[h, rows], s0.at[u], r2.at[u], y, against(h)).start()
 
     def begin(h, _):
         summarize(h, 0)
@@ -288,28 +305,22 @@
     def coef(i, h):
         return ctab[i, pl.ds(h, 1), :]
 
-    STEP = 16
-
     def gather_b(u):
         h, c, rows = unit(u)
-        na, nb, no, nc = path(h)
-
-        @pl.when(z == nb)
-        def _():
-            remote(mem.at[h, rows], land1.at[h, rows], s0.at[u], r1.at[u], y, no).wait_recv()
+        @pl.when(role(h) == 1)
+        def _():
+            remote(mem.at[h, rows], land1.at[h, rows], s0.at[u], r1.at[u], y, along(h)).wait_recv()
             for t in range(ROWS // STEP):
                 part = pl.ds(pl.multiple_of(c * ROWS + t * STEP, STEP), STEP)
                 send1[h, part] = coef(0, h) * land1[h, part] + coef(1, h) * mem[h, part]
-            remote(send1.at[h, rows], land1.at[h, rows], s0.at[u], r1.at[u], y, no).start()
+            remote(send1.at[h, rows], land1.at[h, rows], s0.at[u], r1.at[u], y, along(h)).start()
 
     def own_o(u):
         h, c, rows = unit(u)
-        na, nb, no, nc = path(h)
-
-        @pl.when(z == no)
-        def _():
-            remote(mem.at[h, rows], land1.at[h, rows], s0.at[u], r1.at[u], y, nb).wait_recv()
-            remote(mem.at[h, rows], land2.at[h, rows], s0.at[u], r2.at[u], y, nb).wait_recv()
+        @pl.when(role(h) == 2)
+        def _():
+            remote(mem.at[h, rows], land1.at[h, rows], s0.at[u], r1.at[u], y, along(h)).wait_recv()
+            remote(mem.at[h, rows], land2.at[h, rows], s0.at[u], r2.at[u], y, along(h)).wait_recv()
 
             @pl.when(y == 0)
             def _():
@@ -317,7 +328,7 @@
 
             @pl.when(y > 0)
             def _():
-                remote(mem.at[h, rows], land3.at[h, rows], s0.at[u], r3.at[u], y, nb).wait_recv()
+                remote(mem.at[h, rows], land3.at[h, rows], s0.at[u], r3.at[u], y, along(h)).wait_recv()
 
             for t in range(ROWS // STEP):
                 part = pl.ds(pl.multiple_of(c * ROWS + t * STEP, STEP), STEP)
@@ -338,72 +349,78 @@
             def _():
                 remote(send1.at[h, rows], land3.at[h, rows], s0.at[u], r3.at[u], y + 1, z).start()
 
-            remote(land1.at[h, rows], land3.at[h, rows], s1.at[u], r3.at[u], y, nb).start()
-            remote(land2.at[h, rows], land3.at[h, rows], s2.at[u], r3.at[u], y, nc).start()
+            remote(land1.at[h, rows], land3.at[h, rows], s1.at[u], r3.at[u], y, against(h)).start()
+            remote(land2.at[h, rows], land3.at[h, rows], s2.at[u], r3.at[u], y, along(h)).start()
 
             @pl.when(y == NY - 1)
             def _():
-                for j in range(NZ):
+                for j in range(SHARES):
                     part = pl.ds(pl.multiple_of(c * ROWS + j * STEP, STEP), STEP)
-
-                    @pl.when((c != NY - 1) | (z != j))
+                    to = c * SHARES + j
+
+                    @pl.when(to != me)
                     def _():
-                        remote(send1.at[h, part], fin.at[h], sf.at[u * NZ + j], rf.at[h], c, j).start()
-
-                    @pl.when((c == NY - 1) & (z == j))
+                        remote(
+                            send1.at[h, part], fin.at[h], sf.at[u * SHARES + j], rf.at[h],
+                            jnp.right_shift(to, 2), to & 3,
+                        ).start()
+
+                    @pl.when(to == me)
                     def _():
                         fin[h] = send1[h, part]
 
     def back_b(u):
         h, c, rows = unit(u)
-        na, nb, no, nc = path(h)
-
-        @pl.when(z == nb)
-        def _():
-            remote(mem.at[h, rows], land3.at[h, rows], s0.at[u], r3.at[u], y, no).wait_recv()
+        @pl.when(role(h) == 1)
+        def _():
+            remote(mem.at[h, rows], land3.at[h, rows], s0.at[u], r3.at[u], y, along(h)).wait_recv()
             for t in range(ROWS // STEP):
                 part = pl.ds(pl.multiple_of(c * ROWS + t * STEP, STEP), STEP)
                 zb = land3[h, part]
                 pref[h, part] = (coef(18, h) * zb + coef(19, h) * land1[h, part]).astype(BF16)
                 land3[h, part] = coef(20, h) * zb + coef(21, h) * mem[h, part]
-            remote(land3.at[h, rows], land3.at[h, rows], s1.at[u], r3.at[u], y, na).start()
+            remote(land3.at[h, rows], land3.at[h, rows], s1.at[u], r3.at[u], y, against(h)).start()
 
     def back_e(u):
         h, c, rows = unit(u)
-        na, nb, no, nc = path(h)
-
-        @pl.when((z == na) | (z == nc))
-        def _():
-            remote(mem.at[h, rows], land3.at[h, rows], s0.at[u], r3.at[u], y, nb).wait_recv()
+        @pl.when((role(h) == 0) | (role(h) == 3))
+        def _():
+            remote(mem.at[h, rows], land3.at[h, rows], s0.at[u], r3.at[u], y, along(h)).wait_recv()
             pref[h, rows] = land3[h, rows].astype(BF16)
 
-    def sends_done(u, _):
-        h, c, rows = unit(u)
-        na, nb, no, nc = path(h)
+    def sends_done(h, _):
+        part = role(h)
+        small = pl.ds(0, STEP)
 
         def done(sem):
-            remote(mem.at[h, rows], land1.at[h, rows], sem, r1.at[u], y, nb).wait_send()
-
-        @pl.when((z != no) | (y < NY - 1))
-        def _():
-            done(s0.at[u])
-
-        @pl.when((z == nb) | (z == no))
-        def _():
-            done(s1.at[u])
-
-        @pl.when(z == no)
-        def _():
-            done(s2.at[u])
-
-        @pl.when((z == no) & (y == NY - 1))
-        def _():
-            for j in range(NZ):
-                @pl.when((c != NY - 1) | (z != j))
-                def _():
+            for c in range(PIECES):
+                rows = pl.ds(c * ROWS, ROWS)
+                remote(mem.at[h, rows], land1.at[h, rows], sem.at[h * PIECES + c], r1.at[0], y, along(h)).wait_send()
+
+        @pl.when((part != 2) | (y < NY - 1))
+        def _():
+            done(s0)
+
+        @pl.when((part == 1) | (part == 2))
+        def _():
+            done(s1)
+
+        @pl.when(part == 2)
+        def _():
+            done(s2)
+
+        @pl.when((part == 2) & (y == NY - 1))
+        def _():
+            for i in range(NY * NZ):
+                def one():
                     remote(
-                        mem.at[h, pl.ds(0, STEP)], fin.at[h], sf.at[u * NZ + j], rf.at[h], y, nb
+                        mem.at[h, small], fin.at[h], sf.at[h * NY * NZ + i], rf.at[h], y, along(h)
                     ).wait_send()
+
+                if i < (NY - 1) * NZ:
+                    one()
+                else:
+                    pl.when(z != i - (NY - 1) * NZ)(one)
         return 0
 
     row_id = lax.broadcasted_iota(jnp.int32, (TILE, TILE), 0)
@@ -423,26 +440,21 @@
                 p = jnp.where(row_id >= col_id, p, 0.0)
             den = den + jnp.sum(p, axis=1, keepdims=True)
             total = total + jnp.dot(p.astype(BF16), vs[h, span, :], preferred_element_type=F32)
-        acc[h, i * TILE:(i + 1) * TILE, :] = total
+        w2 = column(cols2, i * TILE, TILE, h, H)
+        acc[h, i * TILE:(i + 1) * TILE, :] = w2 * total
         at = slice(i * TILE, (i + 1) * TILE)
-        dens[at, :] = jnp.where(lane_id == h, den, dens[at, :])
-
-    def finish(h):
-        def tile(i, _):
-            at = pl.ds(pl.multiple_of(i * TILE, TILE), TILE)
-            q = qs[h, at, :]
-            carried_term = jnp.dot(q, pref[h], preferred_element_type=F32)
-            qn = jnp.sum(q.astype(F32) * pnorm[pl.ds(h, 1), :], axis=1, keepdims=True)
-            start = pl.multiple_of(i * TILE, TILE)
-            w1 = column(cols2, start, TILE, h, 0)
-            w2 = column(cols2, start, TILE, h, H)
-            floor = column(cols2, start, TILE, h, 2 * H)
-            den = column(dens, start, TILE, h, 0)
-            bottom = jnp.maximum(jnp.abs(w1 * qn + w2 * den), floor)
-            vs[h, at, :] = ((w1 * carried_term + w2 * acc[h, at, :]) / bottom).astype(BF16)
-            return 0
-
-        lax.fori_loop(0, LEN // TILE, tile, 0)
+        dens[at, :] = jnp.where(lane_id == h, w2 * den, dens[at, :])
+
+    def finish(h, i):
+        at = slice(i * TILE, (i + 1) * TILE)
+        q = qs[h, at, :]
+        qn = jnp.sum(q.astype(F32) * pnorm[pl.ds(h, 1), :], axis=1, keepdims=True)
+        w1 = column(cols2, i * TILE, TILE, h, 0)
+        floor = column(cols2, i * TILE, TILE, h, 2 * H)
+        den = column(dens, i * TILE, TILE, h, 0)
+        inverse = 1.0 / jnp.maximum(jnp.abs(w1 * qn + den), floor)
+        carried_term = jnp.dot(q, pref[h], preferred_element_type=F32)
+        vs[h, at, :] = ((w1 * carried_term + acc[h, at, :]) * inverse).astype(BF16)
 
     lag_o = LAG_O + LAG_Y * y
     lag_b = lag_o + LAG_B
@@ -453,6 +465,8 @@
         def _():
             fn(jnp.clip(u, 0, UNITS - 1))
 
+    lag_f = jnp.maximum(jnp.right_shift(lag_e + PIECES - 1, PIECES.bit_length() - 1), max(H - EARLY + 1, LAG_A)) + 1
+
     def main(hh, _):
         @pl.when(hh + EARLY < H)
         def _():
@@ -461,6 +475,12 @@
         @pl.when(hh == H - EARLY)
         def _():
             spread(norms, snorm, rnorm)
+
+        hf = hh - lag_f
+
+        @pl.when(hf == 0)
+        def _():
+            normals()
 
         for c in range(PIECES):
             v = hh * PIECES + c
@@ -470,37 +490,32 @@
             guarded(back_b, v - lag_b)
             guarded(back_e, v - lag_e)
 
-            @pl.when((hh >= LAG_A) & (hh < H + LAG_A))
-            def _():
-                h = jnp.clip(hh - LAG_A, 0, H - 1)
-                if c == 0:
-                    pltpu.make_async_copy(q_hbm.at[:, 0:DQK], qs.at[h], in_sem.at[2 * H + h]).wait()
-                attend(h, c)
-        hf = hh - jnp.maximum((lag_e + PIECES - 1) // PIECES, max(H - EARLY + 1, LAG_A))
-
-        @pl.when(hf == 0)
-        def _():
-            normals()
-
-        @pl.when((hf >= 0) & (hf < H))
-        def _():
-            finish(jnp.clip(hf, 0, H - 1))
+            if c % EACH == 0:
+                @pl.when((hh >= LAG_A) & (hh < H + LAG_A))
+                def _():
+                    h = jnp.clip(hh - LAG_A, 0, H - 1)
+                    if c == 0:
+                        pltpu.make_async_copy(q_hbm.at[:, 0:DQK], qs.at[h], in_sem.at[2 * H + h]).wait()
+                    attend(h, c // EACH)
+
+            if c % EACH == EACH // 2:
+                @pl.when((hf >= 0) & (hf < H))
+                def _():
+                    finish(jnp.clip(hf, 0, H - 1), c // EACH)
         return 0
 
     max_lag = LAG_O + LAG_Y * (NY - 1) + LAG_B + LAG_E
-    lax.fori_loop(0, H + max((max_lag + PIECES - 1) // PIECES, H - EARLY + 1, LAG_A), main, 0)
+    lax.fori_loop(0, H + max((max_lag + PIECES - 1) // PIECES, H - EARLY + 1, LAG_A) + 1, main, 0)
 
     def last(h, _):
-        na, nb, no, nc = path(h)
-
-        @pl.when((y != NY - 1) | (z != no))
-        def _():
-            remote(mem.at[h, pl.ds(0, STEP)], fin.at[h], s0.at[0], rf.at[h], y, nb).wait_recv()
+        @pl.when((y != NY - 1) | (role(h) != 2))
+        def _():
+            remote(mem.at[h, pl.ds(0, STEP)], fin.at[h], s0.at[0], rf.at[h], y, along(h)).wait_recv()
         finm_ref[h] = fin[h]
         return 0
 
     lax.fori_loop(0, H, last, 0)
-    lax.fori_loop(0, UNITS, sends_done, 0)
+    lax.fori_loop(0, H, sends_done, 0)
     spread_done(stats, sstat, rstat)
     spread_done(norms, snorm, rnorm)
 
@@ -531,7 +546,7 @@
             pltpu.VMEM((H, DQK // ctx, DV), F32),
             pltpu.VMEM((2 * H, 128), F32),
         ),
-        in_specs=[hbm, hbm, hbm, vmem, vmem],
+        in_specs=[hbm] * 5,
         out_specs=(vmem, vmem, vmem),
         scratch_shapes=[
             pltpu.VMEM((H, LEN, DQK), BF16),
@@ -543,6 +558,8 @@
             pltpu.VMEM((H, DQK, DV), F32),
             pltpu.VMEM((H, LEN, DV), F32),
             pltpu.VMEM((H, DQK, DV), BF16),
+            pltpu.VMEM((H, LEN), F32),
+            pltpu.VMEM((H, LEN), F32),
             pltpu.VMEM((LEN, 128), F32),
             pltpu.VMEM((LEN, 128), F32),
             pltpu.VMEM((LEN, 128), F32),
@@ -561,13 +578,13 @@
             dma((UNITS,)),
             dma((UNITS,)),
             dma((UNITS,)),
-            dma((UNITS * NZ,)),
+            dma((UNITS * SHARES,)),
             dma((H,)),
             dma((ctx,)),
             dma((ctx,)),
             dma((ctx,)),
             dma((ctx,)),
-            dma((1,)),
+            dma((2,)),
         ],
         compiler_params=pltpu.CompilerParams(
             collective_id=0, has_side_effects=True, vmem_limit_bytes=57_000_000

time: 108 us -> 105 us (0.972)
  Pallas kernels: 107 us -> 104 us
    pallas_call x1, Pallas kernels: 103 us -> 99.9 us  [shards(): pl.pallas_call(kernel, out_shape=(pltpu.VMEM((H, LEN, DV), BF16), pltpu.V...]
where the time goes in v4:
time: 105 us
  Pallas kernels  104 us (99%)
    pallas_call x1, Pallas kernels, shards(): pl.pallas_call(kernel, out_shape=(pltpu.VMEM((H, LEN, DV), BF16), pltpu.V...  99.9 us
    pallas_call x1, Pallas kernels, shards(): pl.pallas_call(write_out, out_shape=(jax.ShapeDtypeStruct((LEN, H * DV),...  4.02 us

profile of v4, /device:TPU:56, one launch (start us, length us, event | category | flops | bytes accessed | tf_op | source)
XLA Modules:
  0.0 104.5 jit_solution(16523051126498247885)
XLA Ops:
  0.6 99.9 %mlstm_cell.1 = (bf16[8,1024,512]{2,1,0:T(8,128)(2,1)S(1)}, f32[8,16,512]{2,1,0:T(8,128)S(1)}, f32[16,128]{1,0:T(8,128)S(1)}) custom-call(bf16[1024,2048]{1,0:T(8,128)(2,1)} %q_hbm.1, bf16[1024,2048]{1,0:T(8,128)(2,1)} %k_hbm.1, bf16[1024,4096]{1,0:T(8,128)(2,1)} %v_hbm.1, f32[8,1024]{1,0:T(8,128)} %gate_hbm.1, f32[8,1024]{1,0:T(8,128)} %forget_hbm.1), custom_call_target="tpu_custom_call" | custom-call | tf_op jit(solution)/shard_map/mlstm_cell/pallas_call | solution.py:542
  100.5 4.0 %write_out.1 = (bf16[1024,4096]{1,0:T(8,128)(2,1)}, f32[8,16,512]{2,1,0:T(8,128)}, f32[8,16]{1,0:T(8,128)}, f32[8]{0:T(128)}) custom-call(bf16[8,1024,512]{2,1,0:T(8,128)(2,1)S(1)} %get-tuple-element.7.heads, f32[8,16,512]{2,1,0:T(8,128)S(1)} %get-tuple-element.8.finm, f32[16,128]{1,0:T(8,128)S(1)} %get-tuple-element.9.fins), custom_call_target="tpu_custom_call" | custom-call | tf_op jit(solution)/shard_map/write_out/pallas_call | solution.py:594

commit v5 on v4

--- a/solution.py
+++ b/solution.py
@@ -29,7 +29,7 @@
     5: (1, 2, 3, 0),
     6: (1, 0, 3, 2),
 }
-KINDS = (2, 5, 1, 3, 5, 4, 1, 6)
+KINDS = (1, 2, 5, 2, 4, 3, 5, 1, 1, 3, 5, 4, 1, 4, 6, 6)
 ZC = {1: (1, 1, 0), 2: (0, 1, 0), 3: (0, 0, 0), 4: (1, 1, 0), 5: (0, 0, 0), 6: (1, 0, 0)}
 ZB = {1: (0, 1, 0), 2: (0, 1, 1), 3: (0, 1, 1), 4: (0, 0, 0), 5: (0, 0, 1), 6: (0, 0, 0)}
 PO = {1: (0, 0, 0), 2: (0, 0, 0), 3: (0, 0, 1), 4: (1, 0, 0), 5: (1, 0, 1), 6: (1, 0, 1)}
@@ -44,11 +44,11 @@
 TILES = 4
 EACH = PIECES // TILES
 LAG_O = 15
-LAG_Y = 4
-LAG_B = 12
-LAG_E = 9
-LAG_A = 1
-LEAD = 17
+LAG_Y = 1
+LAG_B = 17
+LAG_E = 17
+LAG_A = 0
+LEAD = 15
 EARLY = 8
 NCOEF = 22
 TILE = 256
@@ -154,25 +154,34 @@
 
     spread(stats, sstat, rstat)
 
-    roles = jnp.int32(0)
-    for r in range(NZ):
-        code = sum(PATHS[k].index(r) << (2 * h) for h, k in enumerate(KINDS))
-        roles = jnp.where(z == r, jnp.int32(code), roles)
-    steps = sum(((PATHS[k][1] - PATHS[k][0]) % NZ) << (2 * h) for h, k in enumerate(KINDS))
-
-    def role(h):
-        return jnp.right_shift(roles, 2 * h) & 3
-
-    def along(h):
-        return (z + (jnp.right_shift(jnp.int32(steps), 2 * h) & 3)) & 3
-
-    def against(h):
-        return (z + 4 - (jnp.right_shift(jnp.int32(steps), 2 * h) & 3)) & 3
+    roles = []
+    steps = []
+    for first in (0, H):
+        mine = jnp.int32(0)
+        kinds = KINDS[first:first + H]
+        for r in range(NZ):
+            code = sum(PATHS[k].index(r) << (2 * i) for i, k in enumerate(kinds))
+            mine = jnp.where(z == r, jnp.int32(code), mine)
+        roles.append(mine)
+        steps.append(sum(((PATHS[k][1] - PATHS[k][0]) % NZ) << (2 * i) for i, k in enumerate(kinds)))
+
+    def digit(pair, g):
+        word = jnp.where(g < H, jnp.int32(pair[0]), jnp.int32(pair[1]))
+        return jnp.right_shift(word, 2 * (g & (H - 1))) & 3
+
+    def role(g):
+        return digit(roles, g)
+
+    def along(g):
+        return (z + digit(steps, g)) & 3
+
+    def against(g):
+        return (z + 4 - digit(steps, g)) & 3
 
     def unit(u):
         h = jnp.right_shift(u, PIECES.bit_length() - 1)
         c = u & (PIECES - 1)
-        return h, c, pl.ds(pl.multiple_of(c * ROWS, ROWS), ROWS)
+        return h, jnp.right_shift(u, PIECES.bit_length() - 2), c, pl.ds(pl.multiple_of(c * ROWS, ROWS), ROWS)
 
     def column(table, start, size, h, base):
         x = pltpu.roll(table[pl.ds(start, size), :], lax.rem(128 - h, 128), 1)
@@ -189,16 +198,16 @@
         return 0
 
     def first_send(u):
-        h, c, rows = unit(u)
-        part = role(h)
+        h, g, c, rows = unit(u)
+        part = role(g)
 
         @pl.when(part == 0)
         def _():
-            remote(mem.at[h, rows], land1.at[h, rows], s0.at[u], r1.at[u], y, along(h)).start()
+            remote(mem.at[h, rows], land1.at[h, rows], s0.at[u], r1.at[u], y, along(g)).start()
 
         @pl.when(part == 3)
         def _():
-            remote(mem.at[h, rows], land2.at[h, rows], s0.at[u], r2.at[u], y, against(h)).start()
+            remote(mem.at[h, rows], land2.at[h, rows], s0.at[u], r2.at[u], y, against(g)).start()
 
     def begin(h, _):
         summarize(h, 0)
@@ -212,13 +221,6 @@
 
     gathered(stats, sstat, rstat)
     sub = lax.broadcasted_iota(jnp.int32, (H, 128), 0)
-
-    def by_head(table):
-        out = jnp.zeros((H, 128), F32)
-        for h in range(H):
-            if table[KINDS[h]] != 0:
-                out = jnp.where(sub == h, 1.0, out)
-        return out > 0.5
 
     total = jnp.zeros((H, 128), F32)
     before = jnp.zeros((H, 128), F32)
@@ -242,16 +244,12 @@
             w = jnp.where(y == r, logs[r * NZ + j], w)
         here.append(w)
 
-    def node(i):
-        out = here[0]
-        for j in range(1, NZ):
-            mask = by_head({k: int(PATHS[k][i] == j) for k in PATHS})
-            out = jnp.where(mask, here[j], out)
-        return out
-
-    l_a, l_b, l_o, l_c = (node(i) for i in range(4))
-    l_ab = jnp.maximum(l_a, l_b)
-    coefs = [jnp.exp(l_a - l_ab), jnp.exp(l_b - l_ab)]
+    def by_head(half, table):
+        out = jnp.zeros((H, 128), F32)
+        for h in range(H):
+            if table[KINDS[2 * h + half]] != 0:
+                out = jnp.where(sub == h, 1.0, out)
+        return out > 0.5
 
     def union(base, parts):
         top = base
@@ -263,16 +261,26 @@
             out.append(e if mask is None else jnp.where(mask, e, 0.0))
         return top, out
 
-    coefs += union(top_row, [(l_ab, None), (l_o, None), (l_c, None)])[1]
-    tops = {}
-    for name, table in (("c", ZC), ("b", ZB), ("o", PO)):
-        masks = [by_head({k: table[k][i] for k in table}) for i in range(3)]
-        tops[name], cs = union(top_row, list(zip((l_ab, l_o, l_c), masks)))
-        coefs += cs
-    coefs += union(tops["b"], [(l_a, by_head(PB_A))])[1]
-    coefs += union(tops["b"], [(l_b, by_head(ZA_B))])[1]
-    for i, cf in enumerate(coefs):
-        ctab[i] = jnp.concatenate([cf] * (DV // 128), axis=1)
+    for half in range(2):
+        def node(i):
+            out = here[0]
+            for j in range(1, NZ):
+                out = jnp.where(by_head(half, {k: int(PATHS[k][i] == j) for k in PATHS}), here[j], out)
+            return out
+
+        l_a, l_b, l_o, l_c = (node(i) for i in range(4))
+        l_ab = jnp.maximum(l_a, l_b)
+        coefs = [jnp.exp(l_a - l_ab), jnp.exp(l_b - l_ab)]
+        coefs += union(top_row, [(l_ab, None), (l_o, None), (l_c, None)])[1]
+        tops = {}
+        for name, table in (("c", ZC), ("b", ZB), ("o", PO)):
+            masks = [by_head(half, {k: table[k][i] for k in table}) for i in range(3)]
+            tops[name], cs = union(top_row, list(zip((l_ab, l_o, l_c), masks)))
+            coefs += cs
+        coefs += union(tops["b"], [(l_a, by_head(half, PB_A))])[1]
+        coefs += union(tops["b"], [(l_b, by_head(half, ZA_B))])[1]
+        for i, cf in enumerate(coefs):
+            ctab[half, i] = jnp.concatenate([cf] * (DV // 128), axis=1)
 
     carried = top_me + before
     prefix_top = carried[:, 0:1]
@@ -302,25 +310,25 @@
     def logs_ref(i):
         return logs[i][:, 0:1]
 
-    def coef(i, h):
-        return ctab[i, pl.ds(h, 1), :]
+    def coef(i, h, g):
+        return ctab[g & 1, i, pl.ds(h, 1), :]
 
     def gather_b(u):
-        h, c, rows = unit(u)
-        @pl.when(role(h) == 1)
-        def _():
-            remote(mem.at[h, rows], land1.at[h, rows], s0.at[u], r1.at[u], y, along(h)).wait_recv()
+        h, g, c, rows = unit(u)
+        @pl.when(role(g) == 1)
+        def _():
+            remote(mem.at[h, rows], land1.at[h, rows], s0.at[u], r1.at[u], y, along(g)).wait_recv()
             for t in range(ROWS // STEP):
                 part = pl.ds(pl.multiple_of(c * ROWS + t * STEP, STEP), STEP)
-                send1[h, part] = coef(0, h) * land1[h, part] + coef(1, h) * mem[h, part]
-            remote(send1.at[h, rows], land1.at[h, rows], s0.at[u], r1.at[u], y, along(h)).start()
+                send1[h, part] = coef(0, h, g) * land1[h, part] + coef(1, h, g) * mem[h, part]
+            remote(send1.at[h, rows], land1.at[h, rows], s0.at[u], r1.at[u], y, along(g)).start()
 
     def own_o(u):
-        h, c, rows = unit(u)
-        @pl.when(role(h) == 2)
-        def _():
-            remote(mem.at[h, rows], land1.at[h, rows], s0.at[u], r1.at[u], y, along(h)).wait_recv()
-            remote(mem.at[h, rows], land2.at[h, rows], s0.at[u], r2.at[u], y, along(h)).wait_recv()
+        h, g, c, rows = unit(u)
+        @pl.when(role(g) == 2)
+        def _():
+            remote(mem.at[h, rows], land1.at[h, rows], s0.at[u], r1.at[u], y, along(g)).wait_recv()
+            remote(mem.at[h, rows], land2.at[h, rows], s0.at[u], r2.at[u], y, along(g)).wait_recv()
 
             @pl.when(y == 0)
             def _():
@@ -328,7 +336,7 @@
 
             @pl.when(y > 0)
             def _():
-                remote(mem.at[h, rows], land3.at[h, rows], s0.at[u], r3.at[u], y, along(h)).wait_recv()
+                remote(mem.at[h, rows], land3.at[h, rows], s0.at[u], r3.at[u], y, along(g)).wait_recv()
 
             for t in range(ROWS // STEP):
                 part = pl.ds(pl.multiple_of(c * ROWS + t * STEP, STEP), STEP)
@@ -338,7 +346,7 @@
                 mo = mem[h, part]
 
                 def mix(i):
-                    return coef(i, h) * r + coef(i + 1, h) * xb + coef(i + 2, h) * mo + coef(i + 3, h) * xc
+                    return coef(i, h, g) * r + coef(i + 1, h, g) * xb + coef(i + 2, h, g) * mo + coef(i + 3, h, g) * xc
 
                 send1[h, part] = mix(2)
                 land2[h, part] = mix(6)
@@ -349,8 +357,8 @@
             def _():
                 remote(send1.at[h, rows], land3.at[h, rows], s0.at[u], r3.at[u], y + 1, z).start()
 
-            remote(land1.at[h, rows], land3.at[h, rows], s1.at[u], r3.at[u], y, against(h)).start()
-            remote(land2.at[h, rows], land3.at[h, rows], s2.at[u], r3.at[u], y, along(h)).start()
+            remote(land1.at[h, rows], land3.at[h, rows], s1.at[u], r3.at[u], y, against(g)).start()
+            remote(land2.at[h, rows], land3.at[h, rows], s2.at[u], r3.at[u], y, along(g)).start()
 
             @pl.when(y == NY - 1)
             def _():
@@ -370,32 +378,35 @@
                         fin[h] = send1[h, part]
 
     def back_b(u):
-        h, c, rows = unit(u)
-        @pl.when(role(h) == 1)
-        def _():
-            remote(mem.at[h, rows], land3.at[h, rows], s0.at[u], r3.at[u], y, along(h)).wait_recv()
+        h, g, c, rows = unit(u)
+        @pl.when(role(g) == 1)
+        def _():
+            remote(mem.at[h, rows], land3.at[h, rows], s0.at[u], r3.at[u], y, along(g)).wait_recv()
             for t in range(ROWS // STEP):
                 part = pl.ds(pl.multiple_of(c * ROWS + t * STEP, STEP), STEP)
                 zb = land3[h, part]
-                pref[h, part] = (coef(18, h) * zb + coef(19, h) * land1[h, part]).astype(BF16)
-                land3[h, part] = coef(20, h) * zb + coef(21, h) * mem[h, part]
-            remote(land3.at[h, rows], land3.at[h, rows], s1.at[u], r3.at[u], y, against(h)).start()
+                pref[h, part] = (coef(18, h, g) * zb + coef(19, h, g) * land1[h, part]).astype(BF16)
+                land3[h, part] = coef(20, h, g) * zb + coef(21, h, g) * mem[h, part]
+            remote(land3.at[h, rows], land3.at[h, rows], s1.at[u], r3.at[u], y, against(g)).start()
 
     def back_e(u):
-        h, c, rows = unit(u)
-        @pl.when((role(h) == 0) | (role(h) == 3))
-        def _():
-            remote(mem.at[h, rows], land3.at[h, rows], s0.at[u], r3.at[u], y, along(h)).wait_recv()
+        h, g, c, rows = unit(u)
+        @pl.when((role(g) == 0) | (role(g) == 3))
+        def _():
+            remote(mem.at[h, rows], land3.at[h, rows], s0.at[u], r3.at[u], y, along(g)).wait_recv()
             pref[h, rows] = land3[h, rows].astype(BF16)
 
-    def sends_done(h, _):
-        part = role(h)
+    def sends_done(g, _):
+        part = role(g)
         small = pl.ds(0, STEP)
+        h = jnp.right_shift(g, 1)
 
         def done(sem):
-            for c in range(PIECES):
+            for c in range(PIECES // 2):
                 rows = pl.ds(c * ROWS, ROWS)
-                remote(mem.at[h, rows], land1.at[h, rows], sem.at[h * PIECES + c], r1.at[0], y, along(h)).wait_send()
+                remote(
+                    mem.at[h, rows], land1.at[h, rows], sem.at[g * (PIECES // 2) + c], r1.at[0], y, along(g)
+                ).wait_send()
 
         @pl.when((part != 2) | (y < NY - 1))
         def _():
@@ -411,16 +422,12 @@
 
         @pl.when((part == 2) & (y == NY - 1))
         def _():
-            for i in range(NY * NZ):
-                def one():
+            for i in range(NY * NZ // 2):
+                @pl.when((g & 1) * (NY * NZ // 2) + i != me)
+                def _():
                     remote(
-                        mem.at[h, small], fin.at[h], sf.at[h * NY * NZ + i], rf.at[h], y, along(h)
+                        mem.at[h, small], fin.at[h], sf.at[g * (NY * NZ // 2) + i], rf.at[h], y, along(g)
                     ).wait_send()
-
-                if i < (NY - 1) * NZ:
-                    one()
-                else:
-                    pl.when(z != i - (NY - 1) * NZ)(one)
         return 0
 
     row_id = lax.broadcasted_iota(jnp.int32, (TILE, TILE), 0)
@@ -508,14 +515,16 @@
     lax.fori_loop(0, H + max((max_lag + PIECES - 1) // PIECES, H - EARLY + 1, LAG_A) + 1, main, 0)
 
     def last(h, _):
-        @pl.when((y != NY - 1) | (role(h) != 2))
-        def _():
-            remote(mem.at[h, pl.ds(0, STEP)], fin.at[h], s0.at[0], rf.at[h], y, along(h)).wait_recv()
+        g = 2 * h + jnp.right_shift(me, 3)
+
+        @pl.when((y != NY - 1) | (role(g) != 2))
+        def _():
+            remote(mem.at[h, pl.ds(0, STEP)], fin.at[h], s0.at[0], rf.at[h], y, along(g)).wait_recv()
         finm_ref[h] = fin[h]
         return 0
 
     lax.fori_loop(0, H, last, 0)
-    lax.fori_loop(0, H, sends_done, 0)
+    lax.fori_loop(0, 2 * H, sends_done, 0)
     spread_done(stats, sstat, rstat)
     spread_done(norms, snorm, rnorm)
 
@@ -566,7 +575,7 @@
             pltpu.VMEM((128, LEN), F32),
             pltpu.VMEM((H, LEN), F32),
             pltpu.VMEM((2, H, LEN), F32),
-            pltpu.VMEM((NCOEF, H, DV), F32),
+            pltpu.VMEM((2, NCOEF, H, DV), F32),
             pltpu.VMEM((ctx, 2 * H, 128), F32),
             pltpu.VMEM((ctx, H, DQK), F32),
             pltpu.VMEM((H, DQK), F32),
@@ -587,7 +596,7 @@
             dma((2,)),
         ],
         compiler_params=pltpu.CompilerParams(
-            collective_id=0, has_side_effects=True, vmem_limit_bytes=57_000_000
+            collective_id=0, has_side_effects=True, vmem_limit_bytes=57_000_000, fuse_transposed_lhs_in_matmul=True
         ),
         name="mlstm_cell",
     )(query_matrix, key_vectors, value_vectors, input_gate, forget_gate)

time: 105 us -> 101 us (0.962)
  Pallas kernels: 104 us -> 99.2 us
    pallas_call x1, Pallas kernels: 99.9 us -> 95.2 us  [shards(): pl.pallas_call(kernel, out_shape=(pltpu.VMEM((H, LEN, DV), BF16), pltpu.V...]
where the time goes in v5:
time: 101 us; the launch traced here: 99.8 us
  Pallas kernels  99.2 us (98%)
    pallas_call x1, Pallas kernels, shards(): pl.pallas_call(kernel, out_shape=(pltpu.VMEM((H, LEN, DV), BF16), pltpu.V...  95.2 us
    pallas_call x1, Pallas kernels, shards(): pl.pallas_call(write_out, out_shape=(jax.ShapeDtypeStruct((LEN, H * DV),...  4.02 us

profile of v5, /device:TPU:56, one launch (start us, length us, event | category | flops | bytes accessed | tf_op | source)
XLA Modules:
  0.0 99.8 jit_solution(16659202724348401541)
XLA Ops:
  0.6 95.2 %mlstm_cell.1 = (bf16[8,1024,512]{2,1,0:T(8,128)(2,1)S(1)}, f32[8,16,512]{2,1,0:T(8,128)S(1)}, f32[16,128]{1,0:T(8,128)S(1)}) custom-call(bf16[1024,2048]{1,0:T(8,128)(2,1)} %q_hbm.1, bf16[1024,2048]{1,0:T(8,128)(2,1)} %k_hbm.1, bf16[1024,4096]{1,0:T(8,128)(2,1)} %v_hbm.1, f32[8,1024]{1,0:T(8,128)} %gate_hbm.1, f32[8,1024]{1,0:T(8,128)} %forget_hbm.1), custom_call_target="tpu_custom_call" | custom-call | tf_op jit(solution)/shard_map/mlstm_cell/pallas_call | solution.py:551
  95.8 4.0 %write_out.1 = (bf16[1024,4096]{1,0:T(8,128)(2,1)}, f32[8,16,512]{2,1,0:T(8,128)}, f32[8,16]{1,0:T(8,128)}, f32[8]{0:T(128)}) custom-call(bf16[8,1024,512]{2,1,0:T(8,128)(2,1)S(1)} %get-tuple-element.7.heads, f32[8,16,512]{2,1,0:T(8,128)S(1)} %get-tuple-element.8.finm, f32[16,128]{1,0:T(8,128)S(1)} %get-tuple-element.9.fins), custom_call_target="tpu_custom_call" | custom-call | tf_op jit(solution)/shard_map/write_out/pallas_call | solution.py:603
